TPU v7x, 32 devices: a whole 2x2x4 slice. The times are simulated.
32 devices in a mesh: dp: 1, center: 32 (over z, y, x, core).
Axes of the slice: x: 2, y: 2, z: 4, core: 2. Of those that a mesh axis runs over, the one named last changes fastest.
Arguments:
- embeddings: bfloat16 [1024, 2048], P('dp', 'center'), may hold values from -6 to 6
- first_weight: bfloat16 [2048, 2048], P(None, 'center'), may hold values from -0.125 to 0.125
- first_bias: float32 [2048], P('center'), may hold values from -3 to 3
- second_weight: bfloat16 [2048, 512], P('center'), may hold values from -0.1875 to 0.1875
- centers: bfloat16 [65536, 512], P('center'), may hold values from -4 to 4
- coefficients: bfloat16 [65536, 100], P('center'), may hold values from -12 to 12
- cotangent: bfloat16 [1024, 100], P('dp'), may hold values from -18 to 18
Outputs:
- predictions: float32 [1024, 100], P(('dp', 'center'))
- grad_first: float32 [2048, 2048], P('dp', 'center')
- grad_bias: float32 [2048], P('center')
- grad_second: float32 [2048, 512], P('center', 'dp')
- grad_centers: float32 [65536, 512], P('center', 'dp')
- grad_coefs: float32 [65536, 100], P('center')
All inputs are finite; a program needn't handle non-finite values.
Results may differ from a plain program's by a relative error of at most 0.028.
Values may be sent and summed in bfloat16 or wider, within the bound.
No kernel may reach another device: no remote copies, remote signals or barrier semaphores. Data moves between devices by JAX's collectives and lax.ppermute only.
A program may use at most 64 MiB of HBM per device.

v0:
```python
import jax
import jax.numpy as jnp
from jax import lax
from jax.sharding import PartitionSpec as P


def body(embeddings, first_weight, first_bias, second_weight, centers, coefficients, cotangent):
    feat_width = centers.shape[1]
    factor = 16.0 / feat_width
    gathered = lax.all_gather(embeddings, "center", axis=1, tiled=True)
    preact = jnp.dot(gathered, first_weight, preferred_element_type=jnp.float32) + first_bias
    hidden = jax.nn.gelu(preact).astype(jnp.bfloat16)
    feature_sum = lax.psum(
        jnp.dot(hidden, second_weight, preferred_element_type=jnp.float32), "center"
    )
    squashed = jnp.tanh(feature_sum)
    features = squashed.astype(jnp.bfloat16)
    feat_wide = features.astype(jnp.float32)
    center_wide = centers.astype(jnp.float32)
    feat_norms = jnp.sum(feat_wide * feat_wide, axis=1)
    center_norms = jnp.sum(center_wide * center_wide, axis=1)
    inner_prods = jnp.einsum("tf,cf->tc", features, centers, preferred_element_type=jnp.float32)
    sq_dist = feat_norms[:, None] + center_norms[None, :] - 2.0 * inner_prods
    kernel = jnp.exp(-8.0 * sq_dist / feat_width).astype(jnp.bfloat16)
    pred_part = jnp.dot(kernel, coefficients, preferred_element_type=jnp.float32)
    kernel_grad = jnp.einsum(
        "to,co->tc", cotangent, coefficients, preferred_element_type=jnp.float32
    )
    weighted = kernel_grad * kernel.astype(jnp.float32)
    weighted_low = weighted.astype(jnp.bfloat16)
    feat_grad_part = -factor * (
        jnp.sum(weighted, axis=1)[:, None] * feat_wide
        - jnp.dot(weighted_low, centers, preferred_element_type=jnp.float32)
    )
    center_grad = -factor * (
        jnp.sum(weighted, axis=0)[:, None] * center_wide
        - jnp.einsum("tc,tf->cf", weighted_low, features, preferred_element_type=jnp.float32)
    )
    coef_grad = jnp.einsum("tc,to->co", kernel, cotangent, preferred_element_type=jnp.float32)
    predictions = lax.psum_scatter(
        pred_part.astype(jnp.bfloat16), "center", scatter_dimension=0, tiled=True
    ).astype(jnp.float32)
    feature_grad = lax.psum(feat_grad_part.astype(jnp.bfloat16), "center").astype(jnp.float32)
    phi_grad = (feature_grad * (1.0 - squashed * squashed)).astype(jnp.bfloat16)
    second_grad = jnp.einsum("th,tf->hf", hidden, phi_grad, preferred_element_type=jnp.float32)
    hidden_grad = jnp.einsum(
        "tf,hf->th", phi_grad, second_weight, preferred_element_type=jnp.float32
    )
    unused, pullback = jax.vjp(jax.nn.gelu, preact)
    preact_grad = pullback(hidden_grad)[0]
    bias_grad = jnp.sum(preact_grad, axis=0)
    preact_low = preact_grad.astype(jnp.bfloat16)
    first_grad = jnp.einsum("ti,th->ih", gathered, preact_low, preferred_element_type=jnp.float32)
    first_grad, second_grad, center_grad = (
        lax.psum_scatter(
            first_grad.astype(jnp.bfloat16), "dp", scatter_dimension=0, tiled=True
        ).astype(jnp.float32),
        lax.psum_scatter(
            second_grad.astype(jnp.bfloat16), "dp", scatter_dimension=1, tiled=True
        ).astype(jnp.float32),
        lax.psum_scatter(
            center_grad.astype(jnp.bfloat16), "dp", scatter_dimension=1, tiled=True
        ).astype(jnp.float32),
    )
    bias_grad, coef_grad = (
        lax.psum(bias_grad.astype(jnp.bfloat16), "dp").astype(jnp.float32),
        lax.psum(coef_grad.astype(jnp.bfloat16), "dp").astype(jnp.float32),
    )
    return (predictions, first_grad, bias_grad, second_grad, center_grad, coef_grad)


def solution(mesh):
    placed = (
        P("dp", "center"),
        P(None, "center"),
        P("center"),
        P("center", None),
        P("center", None),
        P("center", None),
        P("dp", None),
    )
    return jax.shard_map(
        body,
        mesh=mesh,
        in_specs=placed,
        out_specs=(
            P(("dp", "center"), None),
            P("dp", "center"),
            P("center"),
            P("center", "dp"),
            P("center", "dp"),
            P("center", None),
        ),
        check_vma=False,
    )
```

profile of v0, /device:TPU:0, one launch (start us, length us, event | category | flops | bytes accessed | tf_op | source)
XLA Modules:
  0.0 502.4 jit_solution(10667676744632239562)
XLA Ops:
  7.2 0.0 copy-start
  7.2 0.0 all-gather.2.cloned.1.call-start
  7.2 0.7 all-gather.2.cloned.1.call-update
  7.9 0.0 copy-start.5
  7.9 0.0 all-reduce.3.cloned.1.call-start
  8.0 67.4 %all-gather.2.cloned.1.call-done = bf16[1024,2048]{0,1:T(8,128)(2,1)} async-done(((bf16[1024,64]{0,1:T(8,128)(2,1)}), bf16[1024,2048]{0,1:T(8,128)(2,1)}) %all-gather.2.cloned.1.call-update) | async-done | bytes 4194320 | tf_op jit(solution)/shard_map/all_gather | solution.py:10
  75.3 3.1 convolution_add_fusion
  78.4 1.8 fusion.25
  80.2 0.0 all-reduce.3.cloned.1.call-update
  80.2 0.0 reduce-scatter.2.cloned.1.call-start
  80.3 0.5 fusion
  80.8 133.9 %all-reduce.3.cloned.1.call-done = f32[1024,512]{1,0:T(8,128)} async-done(((f32[1024,512]{1,0:T(8,128)}), f32[1024,512]{1,0:T(8,128)}) %all-reduce.3.cloned.1.call-update) | async-done | bytes 2097168 | tf_op jit(solution)/shard_map/psum | solution.py:13
  214.7 2.0 fusion.8
  216.7 2.9 exponential_convert_fusion
  219.6 2.0 copy-done.3
  221.6 2.0 convolution_convert_fusion.2
  223.6 0.0 reduce-scatter.2.cloned.1.call-update
  223.6 0.2 all-reduce.5.cloned.1.call-start
  223.8 3.9 fusion.26
  227.7 1.9 copy-done.10
  229.7 3.3 fusion.11
  233.0 0.0 all-reduce.5.cloned.1.call-update
  233.0 7.2 %fusion.4 = f32[2048,512]{1,0:T(8,128)} fusion(bf16[1024,512]{1,0:T(8,128)(2,1)} %copy-done.6, bf16[2048,512]{1,0:T(8,128)(2,1)S(1)} %copy-done.5, f32[2048]{0:T(1024)S(1)} %get-tuple-element.6, bf16[1024,2048]{1,0:T(8,128)(2,1)} %copy-done.10), kind=kOutput, calls=%fused_computation.8 | convolution fusion | flops 2153775104 | bytes 11542528 | tf_op jit(solution)/shard_map/tc,tf->cf/dot_general | solution.py:37
  240.2 1.6 fusion.5
  241.8 116.3 %reduce-scatter.2.cloned.1.call-done = bf16[32,100]{1,0:T(8,128)(2,1)} async-done(((bf16[1024,100]{1,0:T(8,128)(2,1)}), bf16[32,100]{1,0:T(8,128)(2,1)}) %reduce-scatter.2.cloned.1.call-update) | async-done | bytes 6416 | tf_op jit(solution)/shard_map/reduce_scatter | solution.py:40
  358.1 1.3 convert_element_type.79
  359.4 130.3 %all-reduce.5.cloned.1.call-done = bf16[1024,512]{1,0:T(8,128)(2,1)} async-done(((bf16[1024,512]{1,0:T(8,128)(2,1)}), bf16[1024,512]{1,0:T(8,128)(2,1)}) %all-reduce.5.cloned.1.call-update) | async-done | bytes 1048592 | tf_op jit(solution)/shard_map/psum | solution.py:43
  489.7 1.8 multiply_convert_fusion
  491.6 1.0 fusion.17
  492.5 0.6 fusion.27
  493.1 0.5 convert_element_type.160
  493.6 2.2 fusion.7
  (18 shorter events, 0.0 us)
Async XLA Ops:
  7.2 214.4 %copy-start = (bf16[2048,100]{0,1:T(8,128)(2,1)S(1)}, bf16[2048,100]{0,1:T(8,128)(2,1)}, u32[]{:S(2)}) copy-start(bf16[2048,100]{0,1:T(8,128)(2,1)} %param.12) | copy-start | bytes 1228804
  7.2 71.2 %copy-start.9 = (bf16[64,512]{1,0:T(8,128)(2,1)S(1)}, bf16[64,512]{1,0:T(8,128)(2,1)}, u32[]{:S(2)}) copy-start(bf16[64,512]{1,0:T(8,128)(2,1)} %param.10) | copy-start | bytes 196612
  7.2 68.1 %all-gather.2.cloned.1.call-start = ((), (), s32[]{:S(2)}) async-start(), calls=%async_computation.1 | async-start | bytes 4325376 | tf_op jit(solution)/shard_map/all_gather | solution.py:10
  7.9 72.4 %copy-start.5 = (bf16[2048,512]{1,0:T(8,128)(2,1)S(1)}, bf16[2048,512]{1,0:T(8,128)(2,1)}, u32[]{:S(2)}) copy-start(bf16[2048,512]{1,0:T(8,128)(2,1)} %param.11) | copy-start | bytes 6291460
  7.9 206.8 %all-reduce.3.cloned.1.call-start = ((), (), s32[]{:S(2)}) async-start(), calls=%async_computation.2 | async-start | bytes 4194304 | tf_op jit(solution)/shard_map/psum | solution.py:13
  80.2 277.9 %reduce-scatter.2.cloned.1.call-start = ((), (), s32[]{:S(2)}) async-start(), calls=%async_computation.3 | async-start | bytes 270336 | tf_op jit(solution)/shard_map/reduce_scatter | solution.py:40
  216.7 2.9 copy-start.6
  219.6 2.0 copy-start.3
  221.6 2.2 copy-start.8
  223.6 266.1 %all-reduce.5.cloned.1.call-start = ((), (), s32[]{:S(2)}) async-start(), calls=%async_computation.4 | async-start | bytes 2097152 | tf_op jit(solution)/shard_map/psum | solution.py:43
  223.8 5.9 %copy-start.7 = (bf16[1024,512]{1,0:T(8,128)(2,1)S(1)}, bf16[1024,512]{1,0:T(8,128)(2,1)}, u32[]{:S(2)}) copy-start(bf16[1024,512]{1,0:T(8,128)(2,1)} %copy-done.6) | copy-start | bytes 3145732
  227.7 2.0 copy-start.10
  233.0 7.2 %copy-start.4 = (bf16[1024,2048]{1,0:T(8,128)(2,1)S(1)}, bf16[1024,2048]{1,0:T(8,128)(2,1)}, u32[]{:S(2)}) copy-start(bf16[1024,2048]{1,0:T(8,128)(2,1)} %copy-done.3) | copy-start | bytes 12582916
  240.2 249.5 %copy-start.2 = (f32[1024,512]{1,0:T(8,128)S(1)}, f32[1024,512]{1,0:T(8,128)}, u32[]{:S(2)}) copy-start(f32[1024,512]{1,0:T(8,128)} %all-reduce.3.cloned.1.call-done) | copy-start | bytes 6291460
  489.7 3.9 copy-start.1
Sparse Core Ops, SparseCore 0:
  10.9 64.4 all-gather.1
  81.2 133.4 all-reduce.2
  223.7 134.3 reduce-scatter.1
  363.2 126.5 all-reduce.4
where the time goes:
time: 503 us; the launch traced here: 502 us
  waiting for transfers between devices  449 us (89%)
  matrix products  29.4 us (6%)
  between operations  13.9 us (3%)
  other arithmetic  6.12 us (1%)
    psum x1, waiting for transfers between devices, body(): lax.psum(jnp.dot(hidden, second_weight, preferred_element_type=jnp.float3...  134 us
    psum x1, waiting for transfers between devices, body(): lax.psum(feat_grad_part.astype(jnp.bfloat16), 'center').astype(jnp.float32)  130 us
    reduce_scatter x1, waiting for transfers between devices, body(): lax.psum_scatter(pred_part.astype(jnp.bfloat16), 'center', scatter_dimens...  116 us
    all_gather x1, waiting for transfers between devices, body(): gathered = lax.all_gather(embeddings, 'center', axis=1, tiled=True)  67.4 us
  transfers between devices with their start and end apart: 4, of which 4 were waited for; matrix products, arithmetic and copies ran while one was open for 4% of the time, Pallas kernels for 0%

commit v1 on v0

v1 whole, which is shorter than its diff:
```python
import jax
import jax.numpy as jnp
from jax import lax
from jax.sharding import PartitionSpec as P

BF = jnp.bfloat16
F32 = jnp.float32
CORE, X, Y, Z = 1, 2, 4, 8


def pick(bit, zero, one):
    return jnp.where(bit == 1, one, zero)


def ordered(bit, own, other, axis):
    return jnp.concatenate([pick(bit, own, other), pick(bit, other, own)], axis=axis)


def make_body(count, groups):
    deep = count // Z

    def swap(value, bit):
        return lax.ppermute(value, "center", [(i, i ^ bit) for i in range(count)])

    def owner(i):
        block = (i & 1) * 4 + ((i >> 2) & 1) * 2 + ((i >> 1) & 1)
        return deep * block + i // Z

    def body(embeddings, first_weight, first_bias, second_weight, centers, coefficients, cotangent):
        feat_width = centers.shape[1]
        factor = 16.0 / feat_width
        rows = embeddings.shape[0]
        blk = rows // 8
        place = lax.axis_index("center")
        cbit, xbit, ybit, depth = place & 1, (place >> 1) & 1, (place >> 2) & 1, place // Z
        z_bits = [Z << k for k in range(deep.bit_length() - 1)]

        cols = embeddings.shape[1]
        local = embeddings.T
        part = [
            [[local[:, (4 * c + 2 * y + x) * blk:][:, :blk] for x in range(2)] for y in range(2)]
            for c in range(2)
        ]
        cy = [(c, y) for c in range(2) for y in range(2)]
        keep = jnp.concatenate([pick(xbit, part[c][y][0], part[c][y][1]) for c, y in cy], axis=1)
        send = jnp.concatenate([pick(xbit, part[c][y][1], part[c][y][0]) for c, y in cy], axis=1)
        block = ordered(xbit, keep, swap(send, X), 0)
        halves = [[block[:, (2 * c + y) * blk:][:, :blk] for y in range(2)] for c in range(2)]
        keep = jnp.concatenate([pick(ybit, halves[c][0], halves[c][1]) for c in range(2)], axis=1)
        send = jnp.concatenate([pick(ybit, halves[c][1], halves[c][0]) for c in range(2)], axis=1)
        block = ordered(ybit, keep, swap(send, Y), 0)
        for k, bit in enumerate(z_bits):
            block = ordered((depth >> k) & 1, block, swap(block, bit), 0)
        other = swap(block, CORE)
        shape = (4 * deep, 1, cols, 2 * blk)
        emb = ordered(cbit, block.reshape(shape), other.reshape(shape), 1)
        emb = emb.reshape(count * cols, 2 * blk)

        hid = first_weight.shape[1]
        high = first_bias.astype(BF)
        low = (first_bias - high.astype(F32)).astype(BF)
        bias_cols = jnp.pad(jnp.stack([high, low], axis=1), ((0, 0), (0, 126)))
        weights = jnp.concatenate([first_weight.T, second_weight, bias_cols], axis=1)
        weights = jnp.concatenate([weights, swap(weights, X)], axis=0)
        weights = jnp.concatenate([weights, swap(weights, Y)], axis=0)
        din = first_weight.shape[0]
        w_first = weights[:, :din]
        w_second = weights[:, din:din + feat_width]
        bias = weights[:, din + feat_width:][:, :2].astype(F32).sum(axis=1, keepdims=True)

        preact = jnp.dot(w_first, emb, preferred_element_type=F32) + bias
        hidden = jax.nn.gelu(preact).astype(BF)
        part_sum = jnp.einsum("hr,hf->rf", hidden, w_second, preferred_element_type=F32)
        mine = pick(cbit, part_sum[:blk], part_sum[blk:])
        theirs = pick(cbit, part_sum[blk:], part_sum[:blk])
        total = mine + swap(theirs, CORE)

        def deep_sum(value):
            for bit in z_bits:
                low_value = value.astype(BF)
                value = low_value.astype(F32) + swap(low_value, bit).astype(F32)
            return value

        feature_sum = deep_sum(total)
        squashed = jnp.tanh(feature_sum)
        features = squashed.astype(BF)
        for bit in (Y, X, CORE):
            features = jnp.concatenate([features, swap(features, bit)], axis=0)

        cot = cotangent.T
        half, quarter = rows // 2, rows // 4
        cot = pick(cbit, cot, jnp.concatenate([cot[:, half:], cot[:, :half]], axis=1))
        pieces = []
        for c in range(2):
            quad = [cot[:, c * half + i * blk:][:, :blk] for i in range(4)]
            for x in range(2):
                for y in range(2):
                    near = pick(xbit, quad[2 * y + x], quad[2 * y + 1 - x])
                    far = pick(xbit, quad[2 * (1 - y) + x], quad[2 * (1 - y) + 1 - x])
                    pieces.append(pick(ybit, near, far))
        cot = jnp.concatenate(pieces, axis=1)

        feat_wide = features.astype(F32)
        center_wide = centers.astype(F32)
        feat_norms = jnp.sum(feat_wide * feat_wide, axis=1)
        center_norms = jnp.sum(center_wide * center_wide, axis=1)
        inner_prods = jnp.einsum("tf,cf->tc", features, centers, preferred_element_type=F32)
        sq_dist = feat_norms[:, None] + center_norms[None, :] - 2.0 * inner_prods
        kernel = jnp.exp(-8.0 * sq_dist / feat_width).astype(BF)
        pred_part = jnp.dot(kernel, coefficients, preferred_element_type=F32)
        kernel_grad = jnp.einsum("ot,co->tc", cot, coefficients, preferred_element_type=F32)
        weighted = kernel_grad * kernel.astype(F32)
        weighted_low = weighted.astype(BF)
        feat_grad_part = -factor * (
            jnp.sum(weighted, axis=1)[:, None] * feat_wide
            - jnp.dot(weighted_low, centers, preferred_element_type=F32)
        )
        center_grad = -factor * (
            jnp.sum(weighted, axis=0)[:, None] * center_wide
            - jnp.einsum("tc,tf->cf", weighted_low, features, preferred_element_type=F32)
        )
        coef_grad = jnp.einsum("tc,ot->co", kernel, cot, preferred_element_type=F32)

        outs = coefficients.shape[1]
        pred_pad = jnp.pad(pred_part, ((0, 0), (0, -outs % 128)))
        carried = jnp.concatenate([feat_grad_part, pred_pad], axis=1)
        for bit in (CORE, X, Y):
            middle = carried.shape[0] // 2
            carried = carried[:middle] + swap(carried[middle:].astype(BF), bit).astype(F32)
        carried = deep_sum(carried)
        feature_grad = carried[:, :feat_width]
        piece = blk // deep
        mine = lax.dynamic_slice_in_dim(carried[:, feat_width:feat_width + outs], depth * piece, piece, 0)
        predictions = lax.ppermute(
            mine.astype(BF), "center", [(i, owner(i)) for i in range(count)]
        ).astype(F32)

        phi_own = (feature_grad * (1.0 - squashed * squashed)).astype(BF)
        phi_grad = ordered(cbit, phi_own, swap(phi_own, CORE), 0)
        second_grad = jnp.dot(hidden, phi_grad, preferred_element_type=F32)
        hidden_grad = jnp.einsum("hf,rf->hr", w_second, phi_grad, preferred_element_type=F32)
        unused, pullback = jax.vjp(jax.nn.gelu, preact)
        preact_grad = pullback(hidden_grad)[0]
        bias_grad = jnp.sum(preact_grad, axis=1, keepdims=True)
        preact_low = preact_grad.astype(BF)
        first_grad = jnp.einsum("hr,dr->hd", preact_low, emb, preferred_element_type=F32)
        grads = jnp.concatenate(
            [first_grad, second_grad, jnp.pad(bias_grad, ((0, 0), (0, 127)))], axis=1
        )
        for bit in (Y, X):
            middle = grads.shape[0] // 2
            grads = grads[:middle] + swap(grads[middle:].astype(BF), bit).astype(F32)
        first_grad = grads[:, :din].T
        second_grad = grads[:, din:din + feat_width]
        bias_grad = grads[:, din + feat_width]
        if groups > 1:
            first_grad, second_grad, center_grad = (
                lax.psum_scatter(first_grad.astype(BF), "dp", scatter_dimension=0, tiled=True).astype(F32),
                lax.psum_scatter(second_grad.astype(BF), "dp", scatter_dimension=1, tiled=True).astype(F32),
                lax.psum_scatter(center_grad.astype(BF), "dp", scatter_dimension=1, tiled=True).astype(F32),
            )
            bias_grad, coef_grad = (
                lax.psum(bias_grad.astype(BF), "dp").astype(F32),
                lax.psum(coef_grad.astype(BF), "dp").astype(F32),
            )
        return (predictions, first_grad, bias_grad, second_grad, center_grad, coef_grad)

    return body


def solution(mesh):
    placed = (
        P("dp", "center"),
        P(None, "center"),
        P("center"),
        P("center", None),
        P("center", None),
        P("center", None),
        P("dp", None),
    )
    return jax.shard_map(
        make_body(mesh.shape["center"], mesh.shape["dp"]),
        mesh=mesh,
        in_specs=placed,
        out_specs=(
            P(("dp", "center"), None),
            P("dp", "center"),
            P("center"),
            P("center", "dp"),
            P("center", "dp"),
            P("center", None),
        ),
        check_vma=False,
    )
```

time: 503 us -> 146 us (0.29)
  waiting for transfers between devices: 449 us -> 79.3 us
  starting transfers between devices: 0.34 us -> 29.2 us
  between operations: 13.9 us -> 1.14 us
  matrix products: 29.4 us -> 20.5 us
    psum x2 -> x0, waiting for transfers between devices: 264 us -> none  [the longest x1 134 us: body(): lax.psum(jnp.dot(hidden, second_weight, preferred_element_type=jnp.float3...]
    reduce_scatter x1 -> x0, waiting for transfers between devices: 116 us -> none  [body(): lax.psum_scatter(pred_part.astype(jnp.bfloat16), 'center', scatter_dimens...]
    ppermute x0 -> x22, waiting for transfers between devices: none -> 79.3 us  [the longest x21 79.3 us: swap(): return lax.ppermute(value, 'center', [(i, i ^ bit) for i in range(count)])]
    all_gather x1 -> x0, waiting for transfers between devices: 67.4 us -> none  [body(): gathered = lax.all_gather(embeddings, 'center', axis=1, tiled=True)]
    ppermute x0 -> x22, starting transfers between devices: none -> 29.2 us  [the longest x21 28.4 us: swap(): return lax.ppermute(value, 'center', [(i, i ^ bit) for i in range(count)])]
    dot_general x11, matrix products: 29.4 us -> 20.5 us  [the longest x1 4.69 us: body(): jnp.einsum('tc,tf->cf', weighted_low, features, preferred_element_type=F32)]
  transfers between devices with their start and end apart: 4 -> 22, of which waited for: 4 -> 20; matrix products, arithmetic and copies ran while one was open for 4% -> 9% of each run, Pallas kernels for 0% -> 0%
where the time goes in v1:
time: 146 us
  waiting for transfers between devices  79.3 us (54%)
  starting transfers between devices  29.2 us (20%)
  matrix products  20.5 us (14%)
  other arithmetic  9.97 us (7%)
  local copies, waits for them, and re-layouts  5.83 us (4%)
    ppermute x21, waiting for transfers between devices, swap(): return lax.ppermute(value, 'center', [(i, i ^ bit) for i in range(count)])  79.3 us
    ppermute x21, starting transfers between devices, swap(): return lax.ppermute(value, 'center', [(i, i ^ bit) for i in range(count)])  28.4 us
    dot_general x1, matrix products, body(): jnp.einsum('tc,tf->cf', weighted_low, features, preferred_element_type=F32)  4.69 us
    dot_general x1, matrix products, body(): jnp.einsum('tf,cf->tc', features, centers, preferred_element_type=F32)  4.28 us
    select_n x11, other arithmetic, pick(): return jnp.where(bit == 1, one, zero)  3.44 us
  transfers between devices with their start and end apart: 22, of which 20 were waited for; matrix products, arithmetic and copies ran while one was open for 9% of the time, Pallas kernels for 0%

profile of v1, /device:TPU:0, one launch (start us, length us, event | category | flops | bytes accessed | tf_op | source)
XLA Modules:
  0.0 145.9 jit_solution(16864283978115701264)
XLA Ops:
  1.6 3.0 %collective-permute-start.2 = (bf16[64,512]{1,0:T(8,128)(2,1)S(1)}, bf16[64,512]{1,0:T(8,128)(2,1)S(1)}, u32[]{:S(2)}, u32[]{:S(2)}) collective-permute-start(bf16[64,512]{1,0:T(8,128)(2,1)S(1)} %pad_maximum_fusion.16), channel_id=1, source_target_pairs={{0,2},{1,3},{2,0},{3,1},{4,6},{5,7},{6,4},{7,5},{8,10},{9,11},{10,... | collective-permute-start | bytes 196616 | tf_op jit(solution)/shard_map/ppermute | solution.py:23
  7.0 2.1 %collective-permute-start.3 = (bf16[128,256]{1,0:T(8,128)(2,1)S(1)}, bf16[128,256]{1,0:T(8,128)(2,1)S(1)}, u32[]{:S(2)}, u32[]{:S(2)}) collective-permute-start(bf16[128,256]{1,0:T(8,128)(2,1)S(1)} %pad_maximum_fusion.18), channel_id=1, source_target_pairs={{0,4},{1,5},{2,6},{3,7},{4,0},{5,1},{6,2},{7,3},{8,12},{9,13},{10,... | collective-permute-start | bytes 196616 | tf_op jit(solution)/shard_map/ppermute | solution.py:23
  9.2 2.1 %collective-permute-done.3 = bf16[128,256]{1,0:T(8,128)(2,1)S(1)} collective-permute-done((bf16[128,256]{1,0:T(8,128)(2,1)S(1)}, bf16[128,256]{1,0:T(8,128)(2,1)S(1)}, u32[]{:S(2)}, u32[]{:S(2)}) %collective-permute-start.3) | collective-permute-done | bytes 65568 | tf_op jit(solution)/shard_map/ppermute | solution.py:23
  11.4 2.1 %collective-permute-start.4 = (bf16[256,256]{1,0:T(8,128)(2,1)S(1)}, bf16[256,256]{1,0:T(8,128)(2,1)S(1)}, u32[]{:S(2)}, u32[]{:S(2)}) collective-permute-start(bf16[256,256]{1,0:T(8,128)(2,1)S(1)} %pad_maximum_fusion.15), channel_id=1, source_target_pairs={{0,8},{1,9},{2,10},{3,11},{4,12},{5,13},{6,14},{7,15},{8,0},{9,1},... | collective-permute-start | bytes 393224 | tf_op jit(solution)/shard_map/ppermute | solution.py:23
  17.3 3.2 %collective-permute-start.5 = (bf16[512,256]{1,0:T(8,128)(2,1)}, bf16[512,256]{1,0:T(8,128)(2,1)}, u32[]{:S(2)}, u32[]{:S(2)}) collective-permute-start(bf16[512,256]{1,0:T(8,128)(2,1)} %pad_maximum_fusion.8), channel_id=1, source_target_pairs={{0,16},{1,17},{2,18},{3,19},{4,20},{5,21},{6,22},{7,23},{8,24},{9,... | collective-permute-start | bytes 786440 | tf_op jit(solution)/shard_map/ppermute | solution.py:23
  21.9 1.6 %collective-permute-start.1 = (bf16[128,2688]{1,0:T(8,128)(2,1)S(1)}, bf16[128,2688]{1,0:T(8,128)(2,1)S(1)}, u32[]{:S(2)}, u32[]{:S(2)}) collective-permute-start(bf16[128,2688]{1,0:T(8,128)(2,1)S(1)} %pad_maximum_fusion.3), channel_id=1, source_target_pairs={{0,4},{1,5},{2,6},{3,7},{4,0},{5,1},{6,2},{7,3},{8,12},{9,13},{10,... | collective-permute-start | bytes 2064392 | tf_op jit(solution)/shard_map/ppermute | solution.py:23
  23.5 5.6 %collective-permute-done.5 = bf16[512,256]{1,0:T(8,128)(2,1)} collective-permute-done((bf16[512,256]{1,0:T(8,128)(2,1)}, bf16[512,256]{1,0:T(8,128)(2,1)}, u32[]{:S(2)}, u32[]{:S(2)}) %collective-permute-start.5) | collective-permute-done | bytes 262176 | tf_op jit(solution)/shard_map/ppermute | solution.py:23
  31.7 3.8 %collective-permute-done.1 = bf16[128,2688]{1,0:T(8,128)(2,1)S(1)} collective-permute-done((bf16[128,2688]{1,0:T(8,128)(2,1)S(1)}, bf16[128,2688]{1,0:T(8,128)(2,1)S(1)}, u32[]{:S(2)}, u32[]{:S(2)}) %collective-permute-start.1) | collective-permute-done | bytes 688160 | tf_op jit(solution)/shard_map/ppermute | solution.py:23
  41.0 4.7 %collective-permute-done.8 = bf16[128,512]{1,0:T(8,128)(2,1)S(1)} collective-permute-done((bf16[128,512]{1,0:T(8,128)(2,1)S(1)}, bf16[128,512]{1,0:T(8,128)(2,1)S(1)}, u32[]{:S(2)}, u32[]{:S(2)}) %collective-permute-start.8) | collective-permute-done | bytes 131104 | tf_op jit(solution)/shard_map/ppermute | solution.py:23
  45.7 2.7 %collective-permute-start.9 = (bf16[128,512]{1,0:T(8,128)(2,1)S(1)}, bf16[128,512]{1,0:T(8,128)(2,1)S(1)}, u32[]{:S(2)}, u32[]{:S(2)}) collective-permute-start(bf16[128,512]{1,0:T(8,128)(2,1)S(1)} %add_convert_fusion.1), channel_id=1, source_target_pairs={{0,16},{1,17},{2,18},{3,19},{4,20},{5,21},{6,22},{7,23},{8,24},{9,... | collective-permute-start | bytes 393224 | tf_op jit(solution)/shard_map/ppermute | solution.py:23
  48.4 5.8 %collective-permute-done.9 = bf16[128,512]{1,0:T(8,128)(2,1)S(1)} collective-permute-done((bf16[128,512]{1,0:T(8,128)(2,1)S(1)}, bf16[128,512]{1,0:T(8,128)(2,1)S(1)}, u32[]{:S(2)}, u32[]{:S(2)}) %collective-permute-start.9) | collective-permute-done | bytes 131104 | tf_op jit(solution)/shard_map/ppermute | solution.py:23
  54.2 1.6 %collective-permute-start.10 = (bf16[128,512]{1,0:T(8,128)(2,1)S(1)}, bf16[128,512]{1,0:T(8,128)(2,1)S(1)}, u32[]{:S(2)}, u32[]{:S(2)}) collective-permute-start(bf16[128,512]{1,0:T(8,128)(2,1)S(1)} %fusion.20), channel_id=1, source_target_pairs={{0,4},{1,5},{2,6},{3,7},{4,0},{5,1},{6,2},{7,3},{8,12},{9,13},{10,... | collective-permute-start | bytes 393224 | tf_op jit(solution)/shard_map/ppermute | solution.py:23
  55.8 3.6 %collective-permute-done.10 = bf16[128,512]{1,0:T(8,128)(2,1)S(1)} collective-permute-done((bf16[128,512]{1,0:T(8,128)(2,1)S(1)}, bf16[128,512]{1,0:T(8,128)(2,1)S(1)}, u32[]{:S(2)}, u32[]{:S(2)}) %collective-permute-start.10) | collective-permute-done | bytes 131104 | tf_op jit(solution)/shard_map/ppermute | solution.py:23
  59.4 1.7 %collective-permute-start.11 = (bf16[256,512]{1,0:T(8,128)(2,1)S(1)}, bf16[256,512]{1,0:T(8,128)(2,1)S(1)}, u32[]{:S(2)}, u32[]{:S(2)}) collective-permute-start(bf16[256,512]{1,0:T(8,128)(2,1)S(1)} %pad_maximum_fusion.9), channel_id=1, source_target_pairs={{0,2},{1,3},{2,0},{3,1},{4,6},{5,7},{6,4},{7,5},{8,10},{9,11},{10,... | collective-permute-start | bytes 786440 | tf_op jit(solution)/shard_map/ppermute | solution.py:23
  61.1 5.4 %collective-permute-done.11 = bf16[256,512]{1,0:T(8,128)(2,1)S(1)} collective-permute-done((bf16[256,512]{1,0:T(8,128)(2,1)S(1)}, bf16[256,512]{1,0:T(8,128)(2,1)S(1)}, u32[]{:S(2)}, u32[]{:S(2)}) %collective-permute-start.11) | collective-permute-done | bytes 262176 | tf_op jit(solution)/shard_map/ppermute | solution.py:23
  68.8 4.3 %exponential_convert_fusion = bf16[1024,2048]{1,0:T(8,128)(2,1)S(1)} fusion(bf16[2048,512]{1,0:T(8,128)(2,1)S(1)} %copy-done.4, f32[2048]{0:T(1024)S(1)} %fusion, f32[1024]{0:T(1024)S(1)} %fusion.3, bf16[512,512]{1,0:T(8,128)(2,1)S(1)} %collective-permute-done.12, bf16[256,512]{1,0:T(8,128)(2,1)S(1)} %collective-permute-done.11, ...), kind=kOutput, calls=%fused_computation.1 | convolution fusion | flops 2162163712 | bytes 7352320 | tf_op jit(solution)/shard_map/tf,cf->tc/dot_general | solution.py:107
  75.1 1.7 %fusion.31 = (f32[2048]{0:T(1024)S(1)}, f32[1024]{0:T(1024)S(1)}, bf16[1024,2048]{1,0:T(8,128)(2,1)S(1)}) fusion(bf16[1024,2048]{1,0:T(8,128)(2,1)S(1)} %exponential_convert_fusion, bf16[100,1024]{1,0:T(8,128)(2,1)S(1)} %select_dynamic-update-slice_fusion, bf16[2048,100]{0,1:T(8,128)(2,1)S(1)} %copy-done), kind=kOutput, calls=%fused_computation.131 | convolution fusion | flops 429913088 | bytes 9015296 | tf_op jit(solution)/shard_map/ot,co->tc/dot_general | solution.py:111
  76.8 2.3 %fusion.5 = f32[1024,512]{1,0:T(8,128)S(1)} fusion(bf16[2048,512]{1,0:T(8,128)(2,1)S(1)} %copy-done.4, bf16[1024,2048]{1,0:T(8,128)(2,1)S(1)} %get-tuple-element.37, f32[1024]{0:T(1024)S(1)} %get-tuple-element.7, bf16[512,512]{1,0:T(8,128)(2,1)S(1)} %collective-permute-done.12, bf16[256,512]{1,0:T(8,128)(2,1)S(1)} %collective-permute-done.11, ...), kind=kOutput, calls=%fused_computation.15 | convolution fusion | flops 2153250816 | bytes 9441280 | tf_op jit(solution)/shard_map/dot_general | solution.py:116
  79.7 2.0 %collective-permute-done.13 = bf16[512,640]{1,0:T(8,128)(2,1)S(1)} collective-permute-done((bf16[512,640]{1,0:T(8,128)(2,1)S(1)}, bf16[512,640]{1,0:T(8,128)(2,1)S(1)}, u32[]{:S(2)}, u32[]{:S(2)}) %collective-permute-start.13) | collective-permute-done | bytes 655392 | tf_op jit(solution)/shard_map/ppermute | solution.py:23
  81.8 1.7 %collective-permute-start.14 = (bf16[256,640]{1,0:T(8,128)(2,1)S(1)}, bf16[256,640]{1,0:T(8,128)(2,1)S(1)}, u32[]{:S(2)}, u32[]{:S(2)}) collective-permute-start(bf16[256,640]{1,0:T(8,128)(2,1)S(1)} %slice.411), channel_id=1, source_target_pairs={{0,2},{1,3},{2,0},{3,1},{4,6},{5,7},{6,4},{7,5},{8,10},{9,11},{10,... | collective-permute-start | bytes 983048 | tf_op jit(solution)/shard_map/ppermute | solution.py:23
  83.6 8.1 %collective-permute-done.14 = bf16[256,640]{1,0:T(8,128)(2,1)S(1)} collective-permute-done((bf16[256,640]{1,0:T(8,128)(2,1)S(1)}, bf16[256,640]{1,0:T(8,128)(2,1)S(1)}, u32[]{:S(2)}, u32[]{:S(2)}) %collective-permute-start.14) | collective-permute-done | bytes 327712 | tf_op jit(solution)/shard_map/ppermute | solution.py:23
  91.7 1.8 %collective-permute-start.15 = (bf16[128,640]{1,0:T(8,128)(2,1)S(1)}, bf16[128,640]{1,0:T(8,128)(2,1)S(1)}, u32[]{:S(2)}, u32[]{:S(2)}) collective-permute-start(bf16[128,640]{1,0:T(8,128)(2,1)S(1)} %slice.412), channel_id=1, source_target_pairs={{0,4},{1,5},{2,6},{3,7},{4,0},{5,1},{6,2},{7,3},{8,12},{9,13},{10,... | collective-permute-start | bytes 491528 | tf_op jit(solution)/shard_map/ppermute | solution.py:23
  93.5 3.7 %collective-permute-done.15 = bf16[128,640]{1,0:T(8,128)(2,1)S(1)} collective-permute-done((bf16[128,640]{1,0:T(8,128)(2,1)S(1)}, bf16[128,640]{1,0:T(8,128)(2,1)S(1)}, u32[]{:S(2)}, u32[]{:S(2)}) %collective-permute-start.15) | collective-permute-done | bytes 163872 | tf_op jit(solution)/shard_map/ppermute | solution.py:23
  97.3 5.3 %collective-permute-done.16 = bf16[128,640]{1,0:T(8,128)(2,1)S(1)} collective-permute-done((bf16[128,640]{1,0:T(8,128)(2,1)S(1)}, bf16[128,640]{1,0:T(8,128)(2,1)S(1)}, u32[]{:S(2)}, u32[]{:S(2)}) %collective-permute-start.16) | collective-permute-done | bytes 163872 | tf_op jit(solution)/shard_map/ppermute | solution.py:23
  103.1 7.2 %collective-permute-done.17 = bf16[128,640]{1,0:T(8,128)(2,1)S(1)} collective-permute-done((bf16[128,640]{1,0:T(8,128)(2,1)S(1)}, bf16[128,640]{1,0:T(8,128)(2,1)S(1)}, u32[]{:S(2)}, u32[]{:S(2)}) %collective-permute-start.17) | collective-permute-done | bytes 163872 | tf_op jit(solution)/shard_map/ppermute | solution.py:23
  113.1 2.0 %fusion.21 = f32[256,512]{1,0:T(8,128)} fusion(bf16[128,512]{1,0:T(8,128)(2,1)S(1)} %get-tuple-element.15, bf16[128,512]{1,0:T(8,128)(2,1)S(1)} %get-tuple-element.14, f32[256,256]{0,1:T(8,128)} %copy-done.13), kind=kOutput, calls=%fused_computation.67 | convolution fusion | flops 68222976 | bytes 1048576 | tf_op jit(solution)/shard_map/dot_general | solution.py:140
  116.6 1.8 %collective-permute-start.20 = (bf16[128,2688]{1,0:T(8,128)(2,1)S(1)}, bf16[128,2688]{1,0:T(8,128)(2,1)S(1)}, u32[]{:S(2)}, u32[]{:S(2)}) collective-permute-start(bf16[128,2688]{1,0:T(8,128)(2,1)S(1)} %slice.408), channel_id=1, source_target_pairs={{0,4},{1,5},{2,6},{3,7},{4,0},{5,1},{6,2},{7,3},{8,12},{9,13},{10,... | collective-permute-start | bytes 2064392 | tf_op jit(solution)/shard_map/ppermute | solution.py:23
  119.2 4.7 %fusion.2 = f32[2048,512]{1,0:T(8,128)} fusion(bf16[2048,512]{1,0:T(8,128)(2,1)S(1)} %copy-done.5, f32[2048]{0:T(1024)S(1)} %get-tuple-element.6, bf16[1024,2048]{1,0:T(8,128)(2,1)S(1)} %copy-done.15, bf16[512,512]{1,0:T(8,128)(2,1)S(1)} %collective-permute-done.12, bf16[256,512]{1,0:T(8,128)(2,1)S(1)} %collective-permute-done.11, ...), kind=kOutput, calls=%fused_computation.6 | convolution fusion | flops 2155872256 | bytes 11542528 | tf_op jit(solution)/shard_map/tc,tf->cf/dot_general | solution.py:120
  124.7 9.5 %collective-permute-done.20 = bf16[128,2688]{1,0:T(8,128)(2,1)S(1)} collective-permute-done((bf16[128,2688]{1,0:T(8,128)(2,1)S(1)}, bf16[128,2688]{1,0:T(8,128)(2,1)S(1)}, u32[]{:S(2)}, u32[]{:S(2)}) %collective-permute-start.20) | collective-permute-done | bytes 688160 | tf_op jit(solution)/shard_map/ppermute | solution.py:23
  134.4 1.8 %collective-permute-start.21 = (bf16[64,2688]{1,0:T(8,128)(2,1)S(1)}, bf16[64,2688]{1,0:T(8,128)(2,1)S(1)}, u32[]{:S(2)}, u32[]{:S(2)}) collective-permute-start(bf16[64,2688]{1,0:T(8,128)(2,1)S(1)} %slice.410), channel_id=1, source_target_pairs={{0,2},{1,3},{2,0},{3,1},{4,6},{5,7},{6,4},{7,5},{8,10},{9,11},{10,... | collective-permute-start | bytes 1032200 | tf_op jit(solution)/shard_map/ppermute | solution.py:23
  136.1 1.7 %fusion.35 = f32[2048,100]{0,1:T(8,128)} fusion(bf16[1024,2048]{1,0:T(8,128)(2,1)S(1)} %copy-done.2, bf16[100,1024]{1,0:T(8,128)(2,1)S(1)} %copy-done.12), kind=kOutput, calls=%fused_computation.135 | convolution fusion | flops 419430400 | bytes 5218304 | tf_op jit(solution)/shard_map/tc,ot->co/dot_general | solution.py:122
  138.4 5.3 %collective-permute-done.21 = bf16[64,2688]{1,0:T(8,128)(2,1)S(1)} collective-permute-done((bf16[64,2688]{1,0:T(8,128)(2,1)S(1)}, bf16[64,2688]{1,0:T(8,128)(2,1)S(1)}, u32[]{:S(2)}, u32[]{:S(2)}) %collective-permute-start.21) | collective-permute-done | bytes 344096 | tf_op jit(solution)/shard_map/ppermute | solution.py:23
  (119 shorter events, 31.1 us)
Async XLA Ops:
  0.6 72.5 %copy-start = (bf16[2048,100]{0,1:T(8,128)(2,1)S(1)}, bf16[2048,100]{0,1:T(8,128)(2,1)}, u32[]{:S(2)}) copy-start(bf16[2048,100]{0,1:T(8,128)(2,1)} %param.12) | copy-start | bytes 1228804
  0.6 21.2 %copy-start.6 = (bf16[64,512]{1,0:T(8,128)(2,1)S(1)}, bf16[64,512]{1,0:T(8,128)(2,1)}, u32[]{:S(2)}) copy-start(bf16[64,512]{1,0:T(8,128)(2,1)} %param.10) | copy-start | bytes 196612
  0.7 21.2 %copy-start.3 = (bf16[2048,64]{0,1:T(8,128)(2,1)S(1)}, bf16[2048,64]{0,1:T(8,128)(2,1)}, u32[]{:S(2)}) copy-start(bf16[2048,64]{0,1:T(8,128)(2,1)} %param.8) | copy-start | bytes 786436
  1.6 5.3 %collective-permute-start.2 = (bf16[64,512]{1,0:T(8,128)(2,1)S(1)}, bf16[64,512]{1,0:T(8,128)(2,1)S(1)}, u32[]{:S(2)}, u32[]{:S(2)}) collective-permute-start(bf16[64,512]{1,0:T(8,128)(2,1)S(1)} %pad_maximum_fusion.16), channel_id=1, source_target_pairs={{0,2},{1,3},{2,0},{3,1},{4,6},{5,7},{6,4},{7,5},{8,10},{9,11},{10,... | collective-permute-start | bytes 196616 | tf_op jit(solution)/shard_map/ppermute | solution.py:23
  7.0 4.4 %collective-permute-start.3 = (bf16[128,256]{1,0:T(8,128)(2,1)S(1)}, bf16[128,256]{1,0:T(8,128)(2,1)S(1)}, u32[]{:S(2)}, u32[]{:S(2)}) collective-permute-start(bf16[128,256]{1,0:T(8,128)(2,1)S(1)} %pad_maximum_fusion.18), channel_id=1, source_target_pairs={{0,4},{1,5},{2,6},{3,7},{4,0},{5,1},{6,2},{7,3},{8,12},{9,13},{10,... | collective-permute-start | bytes 196616 | tf_op jit(solution)/shard_map/ppermute | solution.py:23
  11.4 5.1 %collective-permute-start.4 = (bf16[256,256]{1,0:T(8,128)(2,1)S(1)}, bf16[256,256]{1,0:T(8,128)(2,1)S(1)}, u32[]{:S(2)}, u32[]{:S(2)}) collective-permute-start(bf16[256,256]{1,0:T(8,128)(2,1)S(1)} %pad_maximum_fusion.15), channel_id=1, source_target_pairs={{0,8},{1,9},{2,10},{3,11},{4,12},{5,13},{6,14},{7,15},{8,0},{9,1},... | collective-permute-start | bytes 393224 | tf_op jit(solution)/shard_map/ppermute | solution.py:23
  14.5 7.3 %collective-permute-start = (bf16[64,2688]{1,0:T(8,128)(2,1)S(1)}, bf16[64,2688]{1,0:T(8,128)(2,1)S(1)}, u32[]{:S(2)}, u32[]{:S(2)}) collective-permute-start(bf16[64,2688]{1,0:T(8,128)(2,1)S(1)} %pad_maximum_fusion.6), channel_id=1, source_target_pairs={{0,2},{1,3},{2,0},{3,1},{4,6},{5,7},{6,4},{7,5},{8,10},{9,11},{10,... | collective-permute-start | bytes 1032200 | tf_op jit(solution)/shard_map/ppermute | solution.py:23
  16.5 14.4 %copy-start.7 = (bf16[1024,100]{0,1:T(8,128)(2,1)S(1)}, bf16[1024,100]{0,1:T(8,128)(2,1)}, u32[]{:S(2)}) copy-start(bf16[1024,100]{0,1:T(8,128)(2,1)} %param.13) | copy-start | bytes 614404
  17.3 11.8 %collective-permute-start.5 = (bf16[512,256]{1,0:T(8,128)(2,1)}, bf16[512,256]{1,0:T(8,128)(2,1)}, u32[]{:S(2)}, u32[]{:S(2)}) collective-permute-start(bf16[512,256]{1,0:T(8,128)(2,1)} %pad_maximum_fusion.8), channel_id=1, source_target_pairs={{0,16},{1,17},{2,18},{3,19},{4,20},{5,21},{6,22},{7,23},{8,24},{9,... | collective-permute-start | bytes 786440 | tf_op jit(solution)/shard_map/ppermute | solution.py:23
  21.9 13.5 %collective-permute-start.1 = (bf16[128,2688]{1,0:T(8,128)(2,1)S(1)}, bf16[128,2688]{1,0:T(8,128)(2,1)S(1)}, u32[]{:S(2)}, u32[]{:S(2)}) collective-permute-start(bf16[128,2688]{1,0:T(8,128)(2,1)S(1)} %pad_maximum_fusion.3), channel_id=1, source_target_pairs={{0,4},{1,5},{2,6},{3,7},{4,0},{5,1},{6,2},{7,3},{8,12},{9,13},{10,... | collective-permute-start | bytes 2064392 | tf_op jit(solution)/shard_map/ppermute | solution.py:23
  31.0 4.7 %collective-permute-start.6 = (bf16[1024,256]{1,0:T(8,128)(2,1)}, bf16[1024,256]{1,0:T(8,128)(2,1)}, u32[]{:S(2)}, u32[]{:S(2)}) collective-permute-start(bf16[1024,256]{1,0:T(8,128)(2,1)} %pad_maximum_fusion.4), channel_id=1, source_target_pairs={{0,1},{1,0},{2,3},{3,2},{4,5},{5,4},{6,7},{7,6},{8,9},{9,8},{10,11... | collective-permute-start | bytes 1572872 | tf_op jit(solution)/shard_map/ppermute | solution.py:23
  38.4 1.6 %collective-permute-start.7 = (f32[128,512]{1,0:T(8,128)S(1)}, f32[128,512]{1,0:T(8,128)S(1)}, u32[]{:S(2)}, u32[]{:S(2)}) collective-permute-start(f32[128,512]{1,0:T(8,128)S(1)} %slice_select_fusion), channel_id=1, source_target_pairs={{0,1},{1,0},{2,3},{3,2},{4,5},{5,4},{6,7},{7,6},{8,9},{9,8},{10,11... | collective-permute-start | bytes 786440 | tf_op jit(solution)/shard_map/ppermute | solution.py:23
  38.6 28.2 %copy-start.4 = (bf16[2048,512]{1,0:T(8,128)(2,1)S(1)}, bf16[2048,512]{1,0:T(8,128)(2,1)}, u32[]{:S(2)}) copy-start(bf16[2048,512]{1,0:T(8,128)(2,1)} %param.11) | copy-start | bytes 6291460
  40.0 5.6 %collective-permute-start.8 = (bf16[128,512]{1,0:T(8,128)(2,1)S(1)}, bf16[128,512]{1,0:T(8,128)(2,1)S(1)}, u32[]{:S(2)}, u32[]{:S(2)}) collective-permute-start(bf16[128,512]{1,0:T(8,128)(2,1)S(1)} %add_convert_fusion.2), channel_id=1, source_target_pairs={{0,8},{1,9},{2,10},{3,11},{4,12},{5,13},{6,14},{7,15},{8,0},{9,1},... | collective-permute-start | bytes 393224 | tf_op jit(solution)/shard_map/ppermute | solution.py:23
  45.7 8.5 %collective-permute-start.9 = (bf16[128,512]{1,0:T(8,128)(2,1)S(1)}, bf16[128,512]{1,0:T(8,128)(2,1)S(1)}, u32[]{:S(2)}, u32[]{:S(2)}) collective-permute-start(bf16[128,512]{1,0:T(8,128)(2,1)S(1)} %add_convert_fusion.1), channel_id=1, source_target_pairs={{0,16},{1,17},{2,18},{3,19},{4,20},{5,21},{6,22},{7,23},{8,24},{9,... | collective-permute-start | bytes 393224 | tf_op jit(solution)/shard_map/ppermute | solution.py:23
  54.2 5.2 %collective-permute-start.10 = (bf16[128,512]{1,0:T(8,128)(2,1)S(1)}, bf16[128,512]{1,0:T(8,128)(2,1)S(1)}, u32[]{:S(2)}, u32[]{:S(2)}) collective-permute-start(bf16[128,512]{1,0:T(8,128)(2,1)S(1)} %fusion.20), channel_id=1, source_target_pairs={{0,4},{1,5},{2,6},{3,7},{4,0},{5,1},{6,2},{7,3},{8,12},{9,13},{10,... | collective-permute-start | bytes 393224 | tf_op jit(solution)/shard_map/ppermute | solution.py:23
  59.4 7.2 %collective-permute-start.11 = (bf16[256,512]{1,0:T(8,128)(2,1)S(1)}, bf16[256,512]{1,0:T(8,128)(2,1)S(1)}, u32[]{:S(2)}, u32[]{:S(2)}) collective-permute-start(bf16[256,512]{1,0:T(8,128)(2,1)S(1)} %pad_maximum_fusion.9), channel_id=1, source_target_pairs={{0,2},{1,3},{2,0},{3,1},{4,6},{5,7},{6,4},{7,5},{8,10},{9,11},{10,... | collective-permute-start | bytes 786440 | tf_op jit(solution)/shard_map/ppermute | solution.py:23
  66.6 2.0 %collective-permute-start.12 = (bf16[512,512]{1,0:T(8,128)(2,1)S(1)}, bf16[512,512]{1,0:T(8,128)(2,1)S(1)}, u32[]{:S(2)}, u32[]{:S(2)}) collective-permute-start(bf16[512,512]{1,0:T(8,128)(2,1)S(1)} %pad_maximum_fusion.5), channel_id=1, source_target_pairs={{0,1},{1,0},{2,3},{3,2},{4,5},{5,4},{6,7},{7,6},{8,9},{9,8},{10,11... | collective-permute-start | bytes 1572872 | tf_op jit(solution)/shard_map/ppermute | solution.py:23
  66.7 7.7 %copy-start.11 = (bf16[100,1024]{1,0:T(8,128)(2,1)}, bf16[100,1024]{1,0:T(8,128)(2,1)S(1)}, u32[]{:S(2)}) copy-start(bf16[100,1024]{1,0:T(8,128)(2,1)S(1)} %select_dynamic-update-slice_fusion) | copy-start | bytes 614404
  76.8 2.4 %copy-start.14 = (bf16[1024,2048]{1,0:T(8,128)(2,1)}, bf16[1024,2048]{1,0:T(8,128)(2,1)S(1)}, u32[]{:S(2)}) copy-start(bf16[1024,2048]{1,0:T(8,128)(2,1)S(1)} %get-tuple-element.37) | copy-start | bytes 12582916
  79.5 2.2 %collective-permute-start.13 = (bf16[512,640]{1,0:T(8,128)(2,1)S(1)}, bf16[512,640]{1,0:T(8,128)(2,1)S(1)}, u32[]{:S(2)}, u32[]{:S(2)}) collective-permute-start(bf16[512,640]{1,0:T(8,128)(2,1)S(1)} %slice.409), channel_id=1, source_target_pairs={{0,1},{1,0},{2,3},{3,2},{4,5},{5,4},{6,7},{7,6},{8,9},{9,8},{10,11... | collective-permute-start | bytes 1966088 | tf_op jit(solution)/shard_map/ppermute | solution.py:23
  81.8 9.8 %collective-permute-start.14 = (bf16[256,640]{1,0:T(8,128)(2,1)S(1)}, bf16[256,640]{1,0:T(8,128)(2,1)S(1)}, u32[]{:S(2)}, u32[]{:S(2)}) collective-permute-start(bf16[256,640]{1,0:T(8,128)(2,1)S(1)} %slice.411), channel_id=1, source_target_pairs={{0,2},{1,3},{2,0},{3,1},{4,6},{5,7},{6,4},{7,5},{8,10},{9,11},{10,... | collective-permute-start | bytes 983048 | tf_op jit(solution)/shard_map/ppermute | solution.py:23
  91.7 5.5 %collective-permute-start.15 = (bf16[128,640]{1,0:T(8,128)(2,1)S(1)}, bf16[128,640]{1,0:T(8,128)(2,1)S(1)}, u32[]{:S(2)}, u32[]{:S(2)}) collective-permute-start(bf16[128,640]{1,0:T(8,128)(2,1)S(1)} %slice.412), channel_id=1, source_target_pairs={{0,4},{1,5},{2,6},{3,7},{4,0},{5,1},{6,2},{7,3},{8,12},{9,13},{10,... | collective-permute-start | bytes 491528 | tf_op jit(solution)/shard_map/ppermute | solution.py:23
  97.2 5.4 %collective-permute-start.16 = (bf16[128,640]{1,0:T(8,128)(2,1)S(1)}, bf16[128,640]{1,0:T(8,128)(2,1)S(1)}, u32[]{:S(2)}, u32[]{:S(2)}) collective-permute-start(bf16[128,640]{1,0:T(8,128)(2,1)S(1)} %fusion.12), channel_id=1, source_target_pairs={{0,8},{1,9},{2,10},{3,11},{4,12},{5,13},{6,14},{7,15},{8,0},{9,1},... | collective-permute-start | bytes 491528 | tf_op jit(solution)/shard_map/ppermute | solution.py:23
  102.7 7.6 %collective-permute-start.17 = (bf16[128,640]{1,0:T(8,128)(2,1)S(1)}, bf16[128,640]{1,0:T(8,128)(2,1)S(1)}, u32[]{:S(2)}, u32[]{:S(2)}) collective-permute-start(bf16[128,640]{1,0:T(8,128)(2,1)S(1)} %add_convert_fusion), channel_id=1, source_target_pairs={{0,16},{1,17},{2,18},{3,19},{4,20},{5,21},{6,22},{7,23},{8,24},{9,... | collective-permute-start | bytes 491528 | tf_op jit(solution)/shard_map/ppermute | solution.py:23
  110.4 1.4 collective-permute-start.19
  116.3 2.8 %copy-start.15 = (bf16[1024,2048]{1,0:T(8,128)(2,1)S(1)}, bf16[1024,2048]{1,0:T(8,128)(2,1)}, u32[]{:S(2)}) copy-start(bf16[1024,2048]{1,0:T(8,128)(2,1)} %copy-done.14) | copy-start | bytes 12582916
  116.6 17.6 %collective-permute-start.20 = (bf16[128,2688]{1,0:T(8,128)(2,1)S(1)}, bf16[128,2688]{1,0:T(8,128)(2,1)S(1)}, u32[]{:S(2)}, u32[]{:S(2)}) collective-permute-start(bf16[128,2688]{1,0:T(8,128)(2,1)S(1)} %slice.408), channel_id=1, source_target_pairs={{0,4},{1,5},{2,6},{3,7},{4,0},{5,1},{6,2},{7,3},{8,12},{9,13},{10,... | collective-permute-start | bytes 2064392 | tf_op jit(solution)/shard_map/ppermute | solution.py:23
  119.2 17.0 %copy-start.12 = (bf16[100,1024]{1,0:T(8,128)(2,1)S(1)}, bf16[100,1024]{1,0:T(8,128)(2,1)}, u32[]{:S(2)}) copy-start(bf16[100,1024]{1,0:T(8,128)(2,1)} %copy-done.11) | copy-start | bytes 614404
  123.8 12.3 %copy-start.2 = (bf16[1024,2048]{1,0:T(8,128)(2,1)S(1)}, bf16[1024,2048]{1,0:T(8,128)(2,1)}, u32[]{:S(2)}) copy-start(bf16[1024,2048]{1,0:T(8,128)(2,1)} %copy-done.1) | copy-start | bytes 12582916
  123.9 13.9 %collective-permute-start.18 = (bf16[32,100]{1,0:T(8,128)(2,1)S(1)}, bf16[32,100]{1,0:T(8,128)(2,1)S(1)}, u32[]{:S(2)}, u32[]{:S(2)}) collective-permute-start(bf16[32,100]{1,0:T(8,128)(2,1)S(1)} %dynamic-slice_convert_fusion), channel_id=1, source_target_pairs={{0,0},{1,16},{2,4},{3,20},{4,8},{5,24},{6,12},{7,28},{8,1},{9,17},... | collective-permute-start | bytes 19208 | tf_op jit(solution)/shard_map/ppermute | solution.py:134
  134.4 9.3 %collective-permute-start.21 = (bf16[64,2688]{1,0:T(8,128)(2,1)S(1)}, bf16[64,2688]{1,0:T(8,128)(2,1)S(1)}, u32[]{:S(2)}, u32[]{:S(2)}) collective-permute-start(bf16[64,2688]{1,0:T(8,128)(2,1)S(1)} %slice.410), channel_id=1, source_target_pairs={{0,2},{1,3},{2,0},{3,1},{4,6},{5,7},{6,4},{7,5},{8,10},{9,11},{10,... | collective-permute-start | bytes 1032200 | tf_op jit(solution)/shard_map/ppermute | solution.py:23
  (6 other events, 8.6 us)

commit v2 on v1

--- a/solution.py
+++ b/solution.py
@@ -14,6 +14,12 @@
 
 def ordered(bit, own, other, axis):
     return jnp.concatenate([pick(bit, own, other), pick(bit, other, own)], axis=axis)
+
+
+def arrange(pieces, bits):
+    for k, bit in enumerate(bits):
+        pieces = [pick(bit, pieces[i], pieces[i ^ (1 << k)]) for i in range(len(pieces))]
+    return pieces
 
 
 def make_body(count, groups):
@@ -35,34 +41,33 @@
         cbit, xbit, ybit, depth = place & 1, (place >> 1) & 1, (place >> 2) & 1, place // Z
         z_bits = [Z << k for k in range(deep.bit_length() - 1)]
 
+        plane = [xbit, ybit]
+
         cols = embeddings.shape[1]
         local = embeddings.T
-        part = [
-            [[local[:, (4 * c + 2 * y + x) * blk:][:, :blk] for x in range(2)] for y in range(2)]
-            for c in range(2)
+        slabs = [
+            jnp.concatenate([local[:, (4 * c + p) * blk:][:, :blk] for c in range(2)], axis=1)
+            for p in range(4)
         ]
-        cy = [(c, y) for c in range(2) for y in range(2)]
-        keep = jnp.concatenate([pick(xbit, part[c][y][0], part[c][y][1]) for c, y in cy], axis=1)
-        send = jnp.concatenate([pick(xbit, part[c][y][1], part[c][y][0]) for c, y in cy], axis=1)
-        block = ordered(xbit, keep, swap(send, X), 0)
-        halves = [[block[:, (2 * c + y) * blk:][:, :blk] for y in range(2)] for c in range(2)]
-        keep = jnp.concatenate([pick(ybit, halves[c][0], halves[c][1]) for c in range(2)], axis=1)
-        send = jnp.concatenate([pick(ybit, halves[c][1], halves[c][0]) for c in range(2)], axis=1)
-        block = ordered(ybit, keep, swap(send, Y), 0)
-        for k, bit in enumerate(z_bits):
-            block = ordered((depth >> k) & 1, block, swap(block, bit), 0)
-        other = swap(block, CORE)
-        shape = (4 * deep, 1, cols, 2 * blk)
-        emb = ordered(cbit, block.reshape(shape), other.reshape(shape), 1)
-        emb = emb.reshape(count * cols, 2 * blk)
+        slabs = arrange(slabs, plane)
+        slabs = [slabs[0]] + [swap(slabs[k], k * X) for k in (3, 1, 2)]
+        slabs = [slabs[0], slabs[2], slabs[3], slabs[1]]
 
         hid = first_weight.shape[1]
         high = first_bias.astype(BF)
         low = (first_bias - high.astype(F32)).astype(BF)
         bias_cols = jnp.pad(jnp.stack([high, low], axis=1), ((0, 0), (0, 126)))
         weights = jnp.concatenate([first_weight.T, second_weight, bias_cols], axis=1)
-        weights = jnp.concatenate([weights, swap(weights, X)], axis=0)
-        weights = jnp.concatenate([weights, swap(weights, Y)], axis=0)
+        weights = jnp.concatenate([weights] + [swap(weights, k * X) for k in (1, 2, 3)], axis=0)
+
+        block = jnp.concatenate(arrange(slabs, plane), axis=0)
+        layers = [block] + [swap(block, k * Z) for k in range(1, deep)]
+        block = jnp.concatenate(arrange(layers, [(depth >> k) & 1 for k in range(len(z_bits))]), axis=0)
+        other = swap(block, CORE)
+        shape = (4 * deep, 1, cols, 2 * blk)
+        emb = ordered(cbit, block.reshape(shape), other.reshape(shape), 1)
+        emb = emb.reshape(count * cols, 2 * blk)
+
         din = first_weight.shape[0]
         w_first = weights[:, :din]
         w_second = weights[:, din:din + feat_width]
@@ -84,21 +89,13 @@
         feature_sum = deep_sum(total)
         squashed = jnp.tanh(feature_sum)
         features = squashed.astype(BF)
-        for bit in (Y, X, CORE):
-            features = jnp.concatenate([features, swap(features, bit)], axis=0)
+        features = jnp.concatenate([features] + [swap(features, k * X) for k in (1, 2, 3)], axis=0)
+        features = jnp.concatenate([features, swap(features, CORE)], axis=0)
 
         cot = cotangent.T
-        half, quarter = rows // 2, rows // 4
-        cot = pick(cbit, cot, jnp.concatenate([cot[:, half:], cot[:, :half]], axis=1))
-        pieces = []
-        for c in range(2):
-            quad = [cot[:, c * half + i * blk:][:, :blk] for i in range(4)]
-            for x in range(2):
-                for y in range(2):
-                    near = pick(xbit, quad[2 * y + x], quad[2 * y + 1 - x])
-                    far = pick(xbit, quad[2 * (1 - y) + x], quad[2 * (1 - y) + 1 - x])
-                    pieces.append(pick(ybit, near, far))
-        cot = jnp.concatenate(pieces, axis=1)
+        cot = jnp.concatenate(
+            arrange([cot[:, i * blk:][:, :blk] for i in range(8)], [xbit, ybit, cbit]), axis=1
+        )
 
         feat_wide = features.astype(F32)
         center_wide = centers.astype(F32)
@@ -121,18 +118,23 @@
         )
         coef_grad = jnp.einsum("tc,ot->co", kernel, cot, preferred_element_type=F32)
 
-        outs = coefficients.shape[1]
-        pred_pad = jnp.pad(pred_part, ((0, 0), (0, -outs % 128)))
-        carried = jnp.concatenate([feat_grad_part, pred_pad], axis=1)
-        for bit in (CORE, X, Y):
-            middle = carried.shape[0] // 2
-            carried = carried[:middle] + swap(carried[middle:].astype(BF), bit).astype(F32)
-        carried = deep_sum(carried)
-        feature_grad = carried[:, :feat_width]
-        piece = blk // deep
-        mine = lax.dynamic_slice_in_dim(carried[:, feat_width:feat_width + outs], depth * piece, piece, 0)
+        def plane_sum(value):
+            middle = value.shape[0] // 2
+            value = value[:middle] + swap(value[middle:].astype(BF), CORE).astype(F32)
+            low_value = value[blk:].astype(BF)
+            parts = [swap(low_value[(k - 1) * blk:][:blk], k * X) for k in (3, 1, 2)]
+            return value[:blk] + sum(part.astype(F32) for part in parts)
+
+        feature_grad = deep_sum(plane_sum(feat_grad_part))
+        preds = plane_sum(pred_part)
+        for k in range(len(z_bits)):
+            middle = preds.shape[0] // 2
+            bit = (depth >> (len(z_bits) - 1 - k)) & 1
+            sent = pick(bit, preds[middle:], preds[:middle]).astype(BF)
+            preds = pick(bit, preds[:middle], preds[middle:])
+            preds = preds + swap(sent, z_bits[len(z_bits) - 1 - k]).astype(F32)
         predictions = lax.ppermute(
-            mine.astype(BF), "center", [(i, owner(i)) for i in range(count)]
+            preds.astype(BF), "center", [(i, owner(i)) for i in range(count)]
         ).astype(F32)
 
         phi_own = (feature_grad * (1.0 - squashed * squashed)).astype(BF)
@@ -143,13 +145,18 @@
         preact_grad = pullback(hidden_grad)[0]
         bias_grad = jnp.sum(preact_grad, axis=1, keepdims=True)
         preact_low = preact_grad.astype(BF)
-        first_grad = jnp.einsum("hr,dr->hd", preact_low, emb, preferred_element_type=F32)
-        grads = jnp.concatenate(
-            [first_grad, second_grad, jnp.pad(bias_grad, ((0, 0), (0, 127)))], axis=1
-        )
-        for bit in (Y, X):
-            middle = grads.shape[0] // 2
-            grads = grads[:middle] + swap(grads[middle:].astype(BF), bit).astype(F32)
+        hid_blk = first_weight.shape[1]
+
+        def head_grads(k):
+            part = slice(k * hid_blk, (k + 1) * hid_blk)
+            return jnp.concatenate([
+                jnp.einsum("hr,dr->hd", preact_low[part], emb, preferred_element_type=F32),
+                second_grad[part],
+                jnp.pad(bias_grad[part], ((0, 0), (0, 127))),
+            ], axis=1)
+
+        received = [swap(head_grads(k).astype(BF), k * X) for k in (3, 1, 2)]
+        grads = head_grads(0) + sum(part.astype(F32) for part in received)
         first_grad = grads[:, :din].T
         second_grad = grads[:, din:din + feat_width]
         bias_grad = grads[:, din + feat_width]

time: 146 us -> 137 us (0.938)
  waiting for transfers between devices: 79.3 us -> 63 us
  starting transfers between devices: 29.2 us -> 40.9 us
  matrix products: 20.5 us -> 18.1 us
    ppermute x21 -> x33, waiting for transfers between devices: 79.3 us -> 63 us  [swap(): return lax.ppermute(value, 'center', [(i, i ^ bit) for i in range(count)])]
    ppermute x21 -> x33, starting transfers between devices: 28.4 us -> 40 us  [swap(): return lax.ppermute(value, 'center', [(i, i ^ bit) for i in range(count)])]
    select_n x11 -> x8, other arithmetic: 3.44 us -> 0.54 us  [pick(): return jnp.where(bit == 1, one, zero)]
    concatenate x9 -> x8, other arithmetic: 0.68 us -> 2.5 us  [the longest x3 2.28 us: head_grads(): jnp.concatenate([jnp.einsum('hr,dr->hd', preact_low[part], emb, preferred...]
    unnamed x7 -> x8, other arithmetic: 0.2 us -> 1.99 us
    dot_general x1, matrix products: 2.04 us -> 0.26 us  [body(): second_grad = jnp.dot(hidden, phi_grad, preferred_element_type=F32)]
    concatenate x4 -> x1, other arithmetic: 1.66 us -> 0.1 us  [ordered(): jnp.concatenate([pick(bit, own, other), pick(bit, other, own)], axis=axis)]
  transfers between devices with their start and end apart: 22 -> 34, of which waited for: 20 -> 18; matrix products, arithmetic and copies ran while one was open for 9% -> 13% of each run, Pallas kernels for 0% -> 0%
where the time goes in v2:
time: 137 us
  waiting for transfers between devices  63 us (46%)
  starting transfers between devices  40.9 us (30%)
  matrix products  18.1 us (13%)
  other arithmetic  8.81 us (6%)
  local copies, waits for them, and re-layouts  5.11 us (4%)
    ppermute x33, waiting for transfers between devices, swap(): return lax.ppermute(value, 'center', [(i, i ^ bit) for i in range(count)])  63 us
    ppermute x33, starting transfers between devices, swap(): return lax.ppermute(value, 'center', [(i, i ^ bit) for i in range(count)])  40 us
    dot_general x1, matrix products, body(): jnp.einsum('tc,tf->cf', weighted_low, features, preferred_element_type=F32)  4.7 us
    dot_general x1, matrix products, body(): jnp.einsum('tf,cf->tc', features, centers, preferred_element_type=F32)  3.13 us
  transfers between devices with their start and end apart: 34, of which 18 were waited for; matrix products, arithmetic and copies ran while one was open for 13% of the time, Pallas kernels for 0%

profile of v2, /device:TPU:0, one launch (start us, length us, event | category | flops | bytes accessed | tf_op | source)
XLA Modules:
  0.0 137.0 jit_solution(17933483423990296759)
XLA Ops:
  2.6 4.0 %collective-permute-start.2 = (bf16[64,2688]{1,0:T(8,128)(2,1)S(1)}, bf16[64,2688]{1,0:T(8,128)(2,1)S(1)}, u32[]{:S(2)}, u32[]{:S(2)}) collective-permute-start(bf16[64,2688]{1,0:T(8,128)(2,1)S(1)} %pad_maximum_fusion.4), channel_id=1, source_target_pairs={{0,6},{1,7},{2,4},{3,5},{4,2},{5,3},{6,0},{7,1},{8,14},{9,15},{10,... | collective-permute-start | bytes 1032200 | tf_op jit(solution)/shard_map/ppermute | solution.py:29
  8.0 1.6 %collective-permute-start.4 = (bf16[64,256]{1,0:T(8,128)(2,1)S(1)}, bf16[64,256]{1,0:T(8,128)(2,1)S(1)}, u32[]{:S(2)}, u32[]{:S(2)}) collective-permute-start(bf16[64,256]{1,0:T(8,128)(2,1)S(1)} %get-tuple-element.36), channel_id=1, source_target_pairs={{0,4},{1,5},{2,6},{3,7},{4,0},{5,1},{6,2},{7,3},{8,12},{9,13},{10,... | collective-permute-start | bytes 98312 | tf_op jit(solution)/shard_map/ppermute | solution.py:29
  10.1 1.5 %collective-permute-start.3 = (bf16[64,256]{1,0:T(8,128)(2,1)S(1)}, bf16[64,256]{1,0:T(8,128)(2,1)S(1)}, u32[]{:S(2)}, u32[]{:S(2)}) collective-permute-start(bf16[64,256]{1,0:T(8,128)(2,1)S(1)} %broadcast_select_fusion.27), channel_id=1, source_target_pairs={{0,6},{1,7},{2,4},{3,5},{4,2},{5,3},{6,0},{7,1},{8,14},{9,15},{10,... | collective-permute-start | bytes 98312 | tf_op jit(solution)/shard_map/ppermute | solution.py:29
  12.5 10.9 %collective-permute-done.4 = bf16[64,256]{1,0:T(8,128)(2,1)S(1)} collective-permute-done((bf16[64,256]{1,0:T(8,128)(2,1)S(1)}, bf16[64,256]{1,0:T(8,128)(2,1)S(1)}, u32[]{:S(2)}, u32[]{:S(2)}) %collective-permute-start.4) | collective-permute-done | bytes 32800 | tf_op jit(solution)/shard_map/ppermute | solution.py:29
  23.5 1.8 %collective-permute-start.8 = (bf16[256,256]{1,0:T(8,128)(2,1)S(1)}, bf16[256,256]{1,0:T(8,128)(2,1)S(1)}, u32[]{:S(2)}, u32[]{:S(2)}) collective-permute-start(bf16[256,256]{1,0:T(8,128)(2,1)S(1)} %pad_maximum_fusion.11), channel_id=1, source_target_pairs={{0,8},{1,9},{2,10},{3,11},{4,12},{5,13},{6,14},{7,15},{8,0},{9,1},... | collective-permute-start | bytes 393224 | tf_op jit(solution)/shard_map/ppermute | solution.py:29
  25.3 2.6 %collective-permute-start.7 = (bf16[256,256]{1,0:T(8,128)(2,1)S(1)}, bf16[256,256]{1,0:T(8,128)(2,1)S(1)}, u32[]{:S(2)}, u32[]{:S(2)}) collective-permute-start(bf16[256,256]{1,0:T(8,128)(2,1)S(1)} %pad_maximum_fusion.11), channel_id=1, source_target_pairs={{0,16},{1,17},{2,18},{3,19},{4,20},{5,21},{6,22},{7,23},{8,24},{9,... | collective-permute-start | bytes 393224 | tf_op jit(solution)/shard_map/ppermute | solution.py:29
  28.8 1.9 %collective-permute-done.8 = bf16[256,256]{1,0:T(8,128)(2,1)S(1)} collective-permute-done((bf16[256,256]{1,0:T(8,128)(2,1)S(1)}, bf16[256,256]{1,0:T(8,128)(2,1)S(1)}, u32[]{:S(2)}, u32[]{:S(2)}) %collective-permute-start.8) | collective-permute-done | bytes 131104 | tf_op jit(solution)/shard_map/ppermute | solution.py:29
  30.7 1.7 %collective-permute-start = (bf16[64,2688]{1,0:T(8,128)(2,1)S(1)}, bf16[64,2688]{1,0:T(8,128)(2,1)S(1)}, u32[]{:S(2)}, u32[]{:S(2)}) collective-permute-start(bf16[64,2688]{1,0:T(8,128)(2,1)S(1)} %pad_maximum_fusion.4), channel_id=1, source_target_pairs={{0,2},{1,3},{2,0},{3,1},{4,6},{5,7},{6,4},{7,5},{8,10},{9,11},{10,... | collective-permute-start | bytes 1032200 | tf_op jit(solution)/shard_map/ppermute | solution.py:29
  32.5 5.7 %collective-permute-done.7 = bf16[256,256]{1,0:T(8,128)(2,1)S(1)} collective-permute-done((bf16[256,256]{1,0:T(8,128)(2,1)S(1)}, bf16[256,256]{1,0:T(8,128)(2,1)S(1)}, u32[]{:S(2)}, u32[]{:S(2)}) %collective-permute-start.7) | collective-permute-done | bytes 131104 | tf_op jit(solution)/shard_map/ppermute | solution.py:29
  38.9 1.6 %collective-permute-done.9 = bf16[1024,256]{1,0:T(8,128)(2,1)S(1)} collective-permute-done((bf16[1024,256]{1,0:T(8,128)(2,1)S(1)}, bf16[1024,256]{1,0:T(8,128)(2,1)S(1)}, u32[]{:S(2)}, u32[]{:S(2)}) %collective-permute-start.9) | collective-permute-done | bytes 524320 | tf_op jit(solution)/shard_map/ppermute | solution.py:29
  43.2 2.2 %collective-permute-start.11 = (bf16[128,512]{1,0:T(8,128)(2,1)S(1)}, bf16[128,512]{1,0:T(8,128)(2,1)S(1)}, u32[]{:S(2)}, u32[]{:S(2)}) collective-permute-start(bf16[128,512]{1,0:T(8,128)(2,1)S(1)} %add_convert_fusion.2), channel_id=1, source_target_pairs={{0,8},{1,9},{2,10},{3,11},{4,12},{5,13},{6,14},{7,15},{8,0},{9,1},... | collective-permute-start | bytes 393224 | tf_op jit(solution)/shard_map/ppermute | solution.py:29
  45.5 3.8 %collective-permute-done.11 = bf16[128,512]{1,0:T(8,128)(2,1)S(1)} collective-permute-done((bf16[128,512]{1,0:T(8,128)(2,1)S(1)}, bf16[128,512]{1,0:T(8,128)(2,1)S(1)}, u32[]{:S(2)}, u32[]{:S(2)}) %collective-permute-start.11) | collective-permute-done | bytes 131104 | tf_op jit(solution)/shard_map/ppermute | solution.py:29
  49.3 2.8 %collective-permute-start.12 = (bf16[128,512]{1,0:T(8,128)(2,1)S(1)}, bf16[128,512]{1,0:T(8,128)(2,1)S(1)}, u32[]{:S(2)}, u32[]{:S(2)}) collective-permute-start(bf16[128,512]{1,0:T(8,128)(2,1)S(1)} %add_convert_fusion.1), channel_id=1, source_target_pairs={{0,16},{1,17},{2,18},{3,19},{4,20},{5,21},{6,22},{7,23},{8,24},{9,... | collective-permute-start | bytes 393224 | tf_op jit(solution)/shard_map/ppermute | solution.py:29
  52.1 5.9 %collective-permute-done.12 = bf16[128,512]{1,0:T(8,128)(2,1)S(1)} collective-permute-done((bf16[128,512]{1,0:T(8,128)(2,1)S(1)}, bf16[128,512]{1,0:T(8,128)(2,1)S(1)}, u32[]{:S(2)}, u32[]{:S(2)}) %collective-permute-start.12) | collective-permute-done | bytes 131104 | tf_op jit(solution)/shard_map/ppermute | solution.py:29
  59.1 2.0 %collective-permute-start.14 = (bf16[128,512]{1,0:T(8,128)(2,1)S(1)}, bf16[128,512]{1,0:T(8,128)(2,1)S(1)}, u32[]{:S(2)}, u32[]{:S(2)}) collective-permute-start(bf16[128,512]{1,0:T(8,128)(2,1)S(1)} %get-tuple-element.35), channel_id=1, source_target_pairs={{0,4},{1,5},{2,6},{3,7},{4,0},{5,1},{6,2},{7,3},{8,12},{9,13},{10,... | collective-permute-start | bytes 393224 | tf_op jit(solution)/shard_map/ppermute | solution.py:29
  61.7 3.3 %collective-permute-done.15 = bf16[128,512]{1,0:T(8,128)(2,1)S(1)} collective-permute-done((bf16[128,512]{1,0:T(8,128)(2,1)S(1)}, bf16[128,512]{1,0:T(8,128)(2,1)S(1)}, u32[]{:S(2)}, u32[]{:S(2)}) %collective-permute-start.15) | collective-permute-done | bytes 131104 | tf_op jit(solution)/shard_map/ppermute | solution.py:29
  66.7 1.8 %collective-permute-done.16 = bf16[512,512]{1,0:T(8,128)(2,1)S(1)} collective-permute-done((bf16[512,512]{1,0:T(8,128)(2,1)S(1)}, bf16[512,512]{1,0:T(8,128)(2,1)S(1)}, u32[]{:S(2)}, u32[]{:S(2)}) %collective-permute-start.16) | collective-permute-done | bytes 524320 | tf_op jit(solution)/shard_map/ppermute | solution.py:29
  68.8 3.1 %exponential_convert_fusion = bf16[1024,2048]{1,0:T(8,128)(2,1)S(1)} fusion(bf16[1024,512]{1,0:T(8,128)(2,1)S(1)} %constant_dynamic-update-slice_fusion, bf16[2048,512]{1,0:T(8,128)(2,1)S(1)} %copy-done.2, f32[2048]{0:T(1024)S(1)} %fusion, f32[1024]{0:T(1024)S(1)} %fusion.3), kind=kOutput, calls=%fused_computation.1 | convolution fusion | flops 2157969408 | bytes 7352320 | tf_op jit(solution)/shard_map/tf,cf->tc/dot_general | solution.py:104
  73.6 1.7 %fusion.37 = (f32[2048]{0:T(1024)S(1)}, f32[1024]{0:T(1024)S(1)}, bf16[1024,2048]{1,0:T(8,128)(2,1)S(1)}) fusion(bf16[1024,2048]{1,0:T(8,128)(2,1)S(1)} %exponential_convert_fusion, bf16[100,1024]{1,0:T(8,128)(2,1)S(1)} %constant_dynamic-update-slice_fusion.5, bf16[2048,100]{0,1:T(8,128)(2,1)S(1)} %copy-done), kind=kOutput, calls=%fused_computation.145 | convolution fusion | flops 429913088 | bytes 9015296 | tf_op jit(solution)/shard_map/ot,co->tc/dot_general | solution.py:108
  75.3 2.3 %fusion.5 = f32[1024,512]{1,0:T(8,128)S(1)} fusion(bf16[1024,512]{1,0:T(8,128)(2,1)S(1)} %constant_dynamic-update-slice_fusion, bf16[2048,512]{1,0:T(8,128)(2,1)S(1)} %copy-done.2, bf16[1024,2048]{1,0:T(8,128)(2,1)S(1)} %get-tuple-element.75, f32[1024]{0:T(1024)S(1)} %get-tuple-element.19), kind=kOutput, calls=%fused_computation.14 | convolution fusion | flops 2149580800 | bytes 9441280 | tf_op jit(solution)/shard_map/dot_general | solution.py:113
  78.2 1.5 %collective-permute-start.18 = (bf16[128,100]{0,1:T(8,128)(2,1)S(1)}, bf16[128,100]{0,1:T(8,128)(2,1)S(1)}, u32[]{:S(2)}, u32[]{:S(2)}) collective-permute-start(bf16[128,100]{0,1:T(8,128)(2,1)S(1)} %get-tuple-element.67), channel_id=1, source_target_pairs={{0,6},{1,7},{2,4},{3,5},{4,2},{5,3},{6,0},{7,1},{8,14},{9,15},{10,... | collective-permute-start | bytes 76808 | tf_op jit(solution)/shard_map/ppermute | solution.py:29
  81.8 4.7 %fusion.2 = f32[2048,512]{1,0:T(8,128)} fusion(bf16[2048,512]{1,0:T(8,128)(2,1)S(1)} %copy-done.2, bf16[1024,512]{1,0:T(8,128)(2,1)S(1)} %constant_dynamic-update-slice_fusion, f32[2048]{0:T(1024)S(1)} %get-tuple-element.18, bf16[1024,2048]{1,0:T(8,128)(2,1)S(1)} %get-tuple-element.75), kind=kOutput, calls=%fused_computation.6 | convolution fusion | flops 2151677952 | bytes 11542528 | tf_op jit(solution)/shard_map/tc,tf->cf/dot_general | solution.py:117
  86.9 1.5 %collective-permute-start.25 = (bf16[128,512]{1,0:T(8,128)(2,1)S(1)}, bf16[128,512]{1,0:T(8,128)(2,1)S(1)}, u32[]{:S(2)}, u32[]{:S(2)}) collective-permute-start(bf16[128,512]{1,0:T(8,128)(2,1)S(1)} %get-tuple-element.41), channel_id=1, source_target_pairs={{0,6},{1,7},{2,4},{3,5},{4,2},{5,3},{6,0},{7,1},{8,14},{9,15},{10,... | collective-permute-start | bytes 393224 | tf_op jit(solution)/shard_map/ppermute | solution.py:29
  91.5 2.5 %collective-permute-done.25 = bf16[128,512]{1,0:T(8,128)(2,1)S(1)} collective-permute-done((bf16[128,512]{1,0:T(8,128)(2,1)S(1)}, bf16[128,512]{1,0:T(8,128)(2,1)S(1)}, u32[]{:S(2)}, u32[]{:S(2)}) %collective-permute-start.25) | collective-permute-done | bytes 131104 | tf_op jit(solution)/shard_map/ppermute | solution.py:29
  95.5 3.0 %collective-permute-start.28 = (bf16[128,512]{1,0:T(8,128)(2,1)S(1)}, bf16[128,512]{1,0:T(8,128)(2,1)S(1)}, u32[]{:S(2)}, u32[]{:S(2)}) collective-permute-start(bf16[128,512]{1,0:T(8,128)(2,1)S(1)} %fusion.25), channel_id=1, source_target_pairs={{0,8},{1,9},{2,10},{3,11},{4,12},{5,13},{6,14},{7,15},{8,0},{9,1},... | collective-permute-start | bytes 393224 | tf_op jit(solution)/shard_map/ppermute | solution.py:29
  98.6 3.1 %collective-permute-done.28 = bf16[128,512]{1,0:T(8,128)(2,1)S(1)} collective-permute-done((bf16[128,512]{1,0:T(8,128)(2,1)S(1)}, bf16[128,512]{1,0:T(8,128)(2,1)S(1)}, u32[]{:S(2)}, u32[]{:S(2)}) %collective-permute-start.28) | collective-permute-done | bytes 131104 | tf_op jit(solution)/shard_map/ppermute | solution.py:29
  101.7 1.5 %collective-permute-start.29 = (bf16[128,512]{1,0:T(8,128)(2,1)S(1)}, bf16[128,512]{1,0:T(8,128)(2,1)S(1)}, u32[]{:S(2)}, u32[]{:S(2)}) collective-permute-start(bf16[128,512]{1,0:T(8,128)(2,1)S(1)} %add_convert_fusion), channel_id=1, source_target_pairs={{0,16},{1,17},{2,18},{3,19},{4,20},{5,21},{6,22},{7,23},{8,24},{9,... | collective-permute-start | bytes 393224 | tf_op jit(solution)/shard_map/ppermute | solution.py:29
  104.2 3.7 %collective-permute-done.29 = bf16[128,512]{1,0:T(8,128)(2,1)S(1)} collective-permute-done((bf16[128,512]{1,0:T(8,128)(2,1)S(1)}, bf16[128,512]{1,0:T(8,128)(2,1)S(1)}, u32[]{:S(2)}, u32[]{:S(2)}) %collective-permute-start.29) | collective-permute-done | bytes 131104 | tf_op jit(solution)/shard_map/ppermute | solution.py:29
  108.1 1.7 %fusion.48 = f32[2048,100]{0,1:T(8,128)} fusion(bf16[1024,2048]{1,0:T(8,128)(2,1)S(1)} %exponential_convert_fusion, bf16[100,1024]{1,0:T(8,128)(2,1)S(1)} %constant_dynamic-update-slice_fusion.5), kind=kOutput, calls=%fused_computation.155 | convolution fusion | flops 419430400 | bytes 5218304 | tf_op jit(solution)/shard_map/tc,ot->co/dot_general | solution.py:119
  113.7 2.6 %collective-permute-start.32 = (bf16[64,2688]{1,0:T(8,128)(2,1)}, bf16[64,2688]{1,0:T(8,128)(2,1)S(1)}, u32[]{:S(2)}, u32[]{:S(2)}) collective-permute-start(bf16[64,2688]{1,0:T(8,128)(2,1)} %fusion.17), channel_id=1, source_target_pairs={{0,2},{1,3},{2,0},{3,1},{4,6},{5,7},{6,4},{7,5},{8,10},{9,11},{10,... | collective-permute-start | bytes 1032200 | tf_op jit(solution)/shard_map/ppermute | solution.py:29
  120.2 5.2 %collective-permute-done.32 = bf16[64,2688]{1,0:T(8,128)(2,1)S(1)} collective-permute-done((bf16[64,2688]{1,0:T(8,128)(2,1)}, bf16[64,2688]{1,0:T(8,128)(2,1)S(1)}, u32[]{:S(2)}, u32[]{:S(2)}) %collective-permute-start.32) | collective-permute-done | bytes 344096 | tf_op jit(solution)/shard_map/ppermute | solution.py:29
  125.4 9.4 %collective-permute-done.33 = bf16[64,2688]{1,0:T(8,128)(2,1)S(1)} collective-permute-done((bf16[64,2688]{1,0:T(8,128)(2,1)}, bf16[64,2688]{1,0:T(8,128)(2,1)S(1)}, u32[]{:S(2)}, u32[]{:S(2)}) %collective-permute-start.33) | collective-permute-done | bytes 344096 | tf_op jit(solution)/shard_map/ppermute | solution.py:29
  (127 shorter events, 33.2 us)
Async XLA Ops:
  2.6 36.0 %collective-permute-start.2 = (bf16[64,2688]{1,0:T(8,128)(2,1)S(1)}, bf16[64,2688]{1,0:T(8,128)(2,1)S(1)}, u32[]{:S(2)}, u32[]{:S(2)}) collective-permute-start(bf16[64,2688]{1,0:T(8,128)(2,1)S(1)} %pad_maximum_fusion.4), channel_id=1, source_target_pairs={{0,6},{1,7},{2,4},{3,5},{4,2},{5,3},{6,0},{7,1},{8,14},{9,15},{10,... | collective-permute-start | bytes 1032200 | tf_op jit(solution)/shard_map/ppermute | solution.py:29
  6.6 32.0 %collective-permute-start.1 = (bf16[64,2688]{1,0:T(8,128)(2,1)S(1)}, bf16[64,2688]{1,0:T(8,128)(2,1)S(1)}, u32[]{:S(2)}, u32[]{:S(2)}) collective-permute-start(bf16[64,2688]{1,0:T(8,128)(2,1)S(1)} %pad_maximum_fusion.4), channel_id=1, source_target_pairs={{0,4},{1,5},{2,6},{3,7},{4,0},{5,1},{6,2},{7,3},{8,12},{9,13},{10,... | collective-permute-start | bytes 1032200 | tf_op jit(solution)/shard_map/ppermute | solution.py:29
  8.0 15.4 %collective-permute-start.4 = (bf16[64,256]{1,0:T(8,128)(2,1)S(1)}, bf16[64,256]{1,0:T(8,128)(2,1)S(1)}, u32[]{:S(2)}, u32[]{:S(2)}) collective-permute-start(bf16[64,256]{1,0:T(8,128)(2,1)S(1)} %get-tuple-element.36), channel_id=1, source_target_pairs={{0,4},{1,5},{2,6},{3,7},{4,0},{5,1},{6,2},{7,3},{8,12},{9,13},{10,... | collective-permute-start | bytes 98312 | tf_op jit(solution)/shard_map/ppermute | solution.py:29
  9.6 13.9 %collective-permute-start.5 = (bf16[64,256]{1,0:T(8,128)(2,1)S(1)}, bf16[64,256]{1,0:T(8,128)(2,1)S(1)}, u32[]{:S(2)}, u32[]{:S(2)}) collective-permute-start(bf16[64,256]{1,0:T(8,128)(2,1)S(1)} %get-tuple-element.58), channel_id=1, source_target_pairs={{0,2},{1,3},{2,0},{3,1},{4,6},{5,7},{6,4},{7,5},{8,10},{9,11},{10,... | collective-permute-start | bytes 98312 | tf_op jit(solution)/shard_map/ppermute | solution.py:29
  10.1 13.3 %collective-permute-start.3 = (bf16[64,256]{1,0:T(8,128)(2,1)S(1)}, bf16[64,256]{1,0:T(8,128)(2,1)S(1)}, u32[]{:S(2)}, u32[]{:S(2)}) collective-permute-start(bf16[64,256]{1,0:T(8,128)(2,1)S(1)} %broadcast_select_fusion.27), channel_id=1, source_target_pairs={{0,6},{1,7},{2,4},{3,5},{4,2},{5,3},{6,0},{7,1},{8,14},{9,15},{10,... | collective-permute-start | bytes 98312 | tf_op jit(solution)/shard_map/ppermute | solution.py:29
  23.5 7.3 %collective-permute-start.8 = (bf16[256,256]{1,0:T(8,128)(2,1)S(1)}, bf16[256,256]{1,0:T(8,128)(2,1)S(1)}, u32[]{:S(2)}, u32[]{:S(2)}) collective-permute-start(bf16[256,256]{1,0:T(8,128)(2,1)S(1)} %pad_maximum_fusion.11), channel_id=1, source_target_pairs={{0,8},{1,9},{2,10},{3,11},{4,12},{5,13},{6,14},{7,15},{8,0},{9,1},... | collective-permute-start | bytes 393224 | tf_op jit(solution)/shard_map/ppermute | solution.py:29
  25.3 12.9 %collective-permute-start.7 = (bf16[256,256]{1,0:T(8,128)(2,1)S(1)}, bf16[256,256]{1,0:T(8,128)(2,1)S(1)}, u32[]{:S(2)}, u32[]{:S(2)}) collective-permute-start(bf16[256,256]{1,0:T(8,128)(2,1)S(1)} %pad_maximum_fusion.11), channel_id=1, source_target_pairs={{0,16},{1,17},{2,18},{3,19},{4,20},{5,21},{6,22},{7,23},{8,24},{9,... | collective-permute-start | bytes 393224 | tf_op jit(solution)/shard_map/ppermute | solution.py:29
  27.9 10.3 %collective-permute-start.6 = (bf16[256,256]{1,0:T(8,128)(2,1)S(1)}, bf16[256,256]{1,0:T(8,128)(2,1)S(1)}, u32[]{:S(2)}, u32[]{:S(2)}) collective-permute-start(bf16[256,256]{1,0:T(8,128)(2,1)S(1)} %pad_maximum_fusion.11), channel_id=1, source_target_pairs={{0,24},{1,25},{2,26},{3,27},{4,28},{5,29},{6,30},{7,31},{8,16},{9,... | collective-permute-start | bytes 393224 | tf_op jit(solution)/shard_map/ppermute | solution.py:29
  30.7 7.8 %collective-permute-start = (bf16[64,2688]{1,0:T(8,128)(2,1)S(1)}, bf16[64,2688]{1,0:T(8,128)(2,1)S(1)}, u32[]{:S(2)}, u32[]{:S(2)}) collective-permute-start(bf16[64,2688]{1,0:T(8,128)(2,1)S(1)} %pad_maximum_fusion.4), channel_id=1, source_target_pairs={{0,2},{1,3},{2,0},{3,1},{4,6},{5,7},{6,4},{7,5},{8,10},{9,11},{10,... | collective-permute-start | bytes 1032200 | tf_op jit(solution)/shard_map/ppermute | solution.py:29
  38.4 2.0 %collective-permute-start.9 = (bf16[1024,256]{1,0:T(8,128)(2,1)S(1)}, bf16[1024,256]{1,0:T(8,128)(2,1)S(1)}, u32[]{:S(2)}, u32[]{:S(2)}) collective-permute-start(bf16[1024,256]{1,0:T(8,128)(2,1)S(1)} %pad_maximum_fusion.2), channel_id=1, source_target_pairs={{0,1},{1,0},{2,3},{3,2},{4,5},{5,4},{6,7},{7,6},{8,9},{9,8},{10,11... | collective-permute-start | bytes 1572872 | tf_op jit(solution)/shard_map/ppermute | solution.py:29
  43.2 6.0 %collective-permute-start.11 = (bf16[128,512]{1,0:T(8,128)(2,1)S(1)}, bf16[128,512]{1,0:T(8,128)(2,1)S(1)}, u32[]{:S(2)}, u32[]{:S(2)}) collective-permute-start(bf16[128,512]{1,0:T(8,128)(2,1)S(1)} %add_convert_fusion.2), channel_id=1, source_target_pairs={{0,8},{1,9},{2,10},{3,11},{4,12},{5,13},{6,14},{7,15},{8,0},{9,1},... | collective-permute-start | bytes 393224 | tf_op jit(solution)/shard_map/ppermute | solution.py:29
  49.3 8.7 %collective-permute-start.12 = (bf16[128,512]{1,0:T(8,128)(2,1)S(1)}, bf16[128,512]{1,0:T(8,128)(2,1)S(1)}, u32[]{:S(2)}, u32[]{:S(2)}) collective-permute-start(bf16[128,512]{1,0:T(8,128)(2,1)S(1)} %add_convert_fusion.1), channel_id=1, source_target_pairs={{0,16},{1,17},{2,18},{3,19},{4,20},{5,21},{6,22},{7,23},{8,24},{9,... | collective-permute-start | bytes 393224 | tf_op jit(solution)/shard_map/ppermute | solution.py:29
  58.1 6.9 %collective-permute-start.15 = (bf16[128,512]{1,0:T(8,128)(2,1)S(1)}, bf16[128,512]{1,0:T(8,128)(2,1)S(1)}, u32[]{:S(2)}, u32[]{:S(2)}) collective-permute-start(bf16[128,512]{1,0:T(8,128)(2,1)S(1)} %get-tuple-element.35), channel_id=1, source_target_pairs={{0,6},{1,7},{2,4},{3,5},{4,2},{5,3},{6,0},{7,1},{8,14},{9,15},{10,... | collective-permute-start | bytes 393224 | tf_op jit(solution)/shard_map/ppermute | solution.py:29
  59.1 7.2 %collective-permute-start.14 = (bf16[128,512]{1,0:T(8,128)(2,1)S(1)}, bf16[128,512]{1,0:T(8,128)(2,1)S(1)}, u32[]{:S(2)}, u32[]{:S(2)}) collective-permute-start(bf16[128,512]{1,0:T(8,128)(2,1)S(1)} %get-tuple-element.35), channel_id=1, source_target_pairs={{0,4},{1,5},{2,6},{3,7},{4,0},{5,1},{6,2},{7,3},{8,12},{9,13},{10,... | collective-permute-start | bytes 393224 | tf_op jit(solution)/shard_map/ppermute | solution.py:29
  61.1 5.4 %collective-permute-start.13 = (bf16[128,512]{1,0:T(8,128)(2,1)S(1)}, bf16[128,512]{1,0:T(8,128)(2,1)S(1)}, u32[]{:S(2)}, u32[]{:S(2)}) collective-permute-start(bf16[128,512]{1,0:T(8,128)(2,1)S(1)} %get-tuple-element.35), channel_id=1, source_target_pairs={{0,2},{1,3},{2,0},{3,1},{4,6},{5,7},{6,4},{7,5},{8,10},{9,11},{10,... | collective-permute-start | bytes 393224 | tf_op jit(solution)/shard_map/ppermute | solution.py:29
  73.4 4.8 %collective-permute-start.17 = (bf16[512,100]{0,1:T(8,128)(2,1)S(1)}, bf16[512,100]{0,1:T(8,128)(2,1)S(1)}, u32[]{:S(2)}, u32[]{:S(2)}) collective-permute-start(bf16[512,100]{0,1:T(8,128)(2,1)S(1)} %slice.377), channel_id=1, source_target_pairs={{0,1},{1,0},{2,3},{3,2},{4,5},{5,4},{6,7},{7,6},{8,9},{9,8},{10,11... | collective-permute-start | bytes 307208 | tf_op jit(solution)/shard_map/ppermute | solution.py:29
  77.7 8.9 %collective-permute-start.24 = (bf16[512,512]{1,0:T(8,128)(2,1)S(1)}, bf16[512,512]{1,0:T(8,128)(2,1)S(1)}, u32[]{:S(2)}, u32[]{:S(2)}) collective-permute-start(bf16[512,512]{1,0:T(8,128)(2,1)S(1)} %slice.376), channel_id=1, source_target_pairs={{0,1},{1,0},{2,3},{3,2},{4,5},{5,4},{6,7},{7,6},{8,9},{9,8},{10,11... | collective-permute-start | bytes 1572872 | tf_op jit(solution)/shard_map/ppermute | solution.py:29
  78.2 8.3 %collective-permute-start.18 = (bf16[128,100]{0,1:T(8,128)(2,1)S(1)}, bf16[128,100]{0,1:T(8,128)(2,1)S(1)}, u32[]{:S(2)}, u32[]{:S(2)}) collective-permute-start(bf16[128,100]{0,1:T(8,128)(2,1)S(1)} %get-tuple-element.67), channel_id=1, source_target_pairs={{0,6},{1,7},{2,4},{3,5},{4,2},{5,3},{6,0},{7,1},{8,14},{9,15},{10,... | collective-permute-start | bytes 76808 | tf_op jit(solution)/shard_map/ppermute | solution.py:29
  79.8 6.7 %collective-permute-start.20 = (bf16[128,100]{0,1:T(8,128)(2,1)S(1)}, bf16[128,100]{0,1:T(8,128)(2,1)S(1)}, u32[]{:S(2)}, u32[]{:S(2)}) collective-permute-start(bf16[128,100]{0,1:T(8,128)(2,1)S(1)} %get-tuple-element.68), channel_id=1, source_target_pairs={{0,4},{1,5},{2,6},{3,7},{4,0},{5,1},{6,2},{7,3},{8,12},{9,13},{10,... | collective-permute-start | bytes 76808 | tf_op jit(solution)/shard_map/ppermute | solution.py:29
  81.2 5.3 %collective-permute-start.19 = (bf16[128,100]{0,1:T(8,128)(2,1)S(1)}, bf16[128,100]{0,1:T(8,128)(2,1)S(1)}, u32[]{:S(2)}, u32[]{:S(2)}) collective-permute-start(bf16[128,100]{0,1:T(8,128)(2,1)S(1)} %get-tuple-element.69), channel_id=1, source_target_pairs={{0,2},{1,3},{2,0},{3,1},{4,6},{5,7},{6,4},{7,5},{8,10},{9,11},{10,... | collective-permute-start | bytes 76808 | tf_op jit(solution)/shard_map/ppermute | solution.py:29
  86.6 4.8 %collective-permute-start.21 = (bf16[64,100]{0,1:T(8,128)(2,1)S(1)}, bf16[64,100]{0,1:T(8,128)(2,1)S(1)}, u32[]{:S(2)}, u32[]{:S(2)}) collective-permute-start(bf16[64,100]{0,1:T(8,128)(2,1)S(1)} %select_convert_fusion.1), channel_id=1, source_target_pairs={{0,16},{1,17},{2,18},{3,19},{4,20},{5,21},{6,22},{7,23},{8,24},{9,... | collective-permute-start | bytes 38408 | tf_op jit(solution)/shard_map/ppermute | solution.py:29
  86.9 7.2 %collective-permute-start.25 = (bf16[128,512]{1,0:T(8,128)(2,1)S(1)}, bf16[128,512]{1,0:T(8,128)(2,1)S(1)}, u32[]{:S(2)}, u32[]{:S(2)}) collective-permute-start(bf16[128,512]{1,0:T(8,128)(2,1)S(1)} %get-tuple-element.41), channel_id=1, source_target_pairs={{0,6},{1,7},{2,4},{3,5},{4,2},{5,3},{6,0},{7,1},{8,14},{9,15},{10,... | collective-permute-start | bytes 393224 | tf_op jit(solution)/shard_map/ppermute | solution.py:29
  88.5 6.9 %collective-permute-start.27 = (bf16[128,512]{1,0:T(8,128)(2,1)S(1)}, bf16[128,512]{1,0:T(8,128)(2,1)S(1)}, u32[]{:S(2)}, u32[]{:S(2)}) collective-permute-start(bf16[128,512]{1,0:T(8,128)(2,1)S(1)} %get-tuple-element.42), channel_id=1, source_target_pairs={{0,4},{1,5},{2,6},{3,7},{4,0},{5,1},{6,2},{7,3},{8,12},{9,13},{10,... | collective-permute-start | bytes 393224 | tf_op jit(solution)/shard_map/ppermute | solution.py:29
  89.8 5.5 %collective-permute-start.26 = (bf16[128,512]{1,0:T(8,128)(2,1)S(1)}, bf16[128,512]{1,0:T(8,128)(2,1)S(1)}, u32[]{:S(2)}, u32[]{:S(2)}) collective-permute-start(bf16[128,512]{1,0:T(8,128)(2,1)S(1)} %get-tuple-element.43), channel_id=1, source_target_pairs={{0,2},{1,3},{2,0},{3,1},{4,6},{5,7},{6,4},{7,5},{8,10},{9,11},{10,... | collective-permute-start | bytes 393224 | tf_op jit(solution)/shard_map/ppermute | solution.py:29
  95.5 6.2 %collective-permute-start.28 = (bf16[128,512]{1,0:T(8,128)(2,1)S(1)}, bf16[128,512]{1,0:T(8,128)(2,1)S(1)}, u32[]{:S(2)}, u32[]{:S(2)}) collective-permute-start(bf16[128,512]{1,0:T(8,128)(2,1)S(1)} %fusion.25), channel_id=1, source_target_pairs={{0,8},{1,9},{2,10},{3,11},{4,12},{5,13},{6,14},{7,15},{8,0},{9,1},... | collective-permute-start | bytes 393224 | tf_op jit(solution)/shard_map/ppermute | solution.py:29
  98.5 4.7 %collective-permute-start.22 = (bf16[32,100]{0,1:T(8,128)(2,1)S(1)}, bf16[32,100]{0,1:T(8,128)(2,1)S(1)}, u32[]{:S(2)}, u32[]{:S(2)}) collective-permute-start(bf16[32,100]{0,1:T(8,128)(2,1)S(1)} %select_convert_fusion), channel_id=1, source_target_pairs={{0,8},{1,9},{2,10},{3,11},{4,12},{5,13},{6,14},{7,15},{8,0},{9,1},... | collective-permute-start | bytes 19208 | tf_op jit(solution)/shard_map/ppermute | solution.py:29
  101.7 6.2 %collective-permute-start.29 = (bf16[128,512]{1,0:T(8,128)(2,1)S(1)}, bf16[128,512]{1,0:T(8,128)(2,1)S(1)}, u32[]{:S(2)}, u32[]{:S(2)}) collective-permute-start(bf16[128,512]{1,0:T(8,128)(2,1)S(1)} %add_convert_fusion), channel_id=1, source_target_pairs={{0,16},{1,17},{2,18},{3,19},{4,20},{5,21},{6,22},{7,23},{8,24},{9,... | collective-permute-start | bytes 393224 | tf_op jit(solution)/shard_map/ppermute | solution.py:29
  103.3 6.4 %collective-permute-start.23 = (bf16[32,100]{0,1:T(8,128)(2,1)S(1)}, bf16[32,100]{0,1:T(8,128)(2,1)S(1)}, u32[]{:S(2)}, u32[]{:S(2)}) collective-permute-start(bf16[32,100]{0,1:T(8,128)(2,1)S(1)} %add_convert_fusion.3), channel_id=1, source_target_pairs={{0,0},{1,16},{2,4},{3,20},{4,8},{5,24},{6,12},{7,28},{8,1},{9,17},... | collective-permute-start | bytes 19208 | tf_op jit(solution)/shard_map/ppermute | solution.py:136
  108.0 2.4 %collective-permute-start.30 = (bf16[128,512]{1,0:T(8,128)(2,1)S(1)}, bf16[128,512]{1,0:T(8,128)(2,1)S(1)}, u32[]{:S(2)}, u32[]{:S(2)}) collective-permute-start(bf16[128,512]{1,0:T(8,128)(2,1)S(1)} %multiply_convert_fusion), channel_id=1, source_target_pairs={{0,1},{1,0},{2,3},{3,2},{4,5},{5,4},{6,7},{7,6},{8,9},{9,8},{10,11... | collective-permute-start | bytes 393224 | tf_op jit(solution)/shard_map/ppermute | solution.py:29
  113.7 11.7 %collective-permute-start.32 = (bf16[64,2688]{1,0:T(8,128)(2,1)}, bf16[64,2688]{1,0:T(8,128)(2,1)S(1)}, u32[]{:S(2)}, u32[]{:S(2)}) collective-permute-start(bf16[64,2688]{1,0:T(8,128)(2,1)} %fusion.17), channel_id=1, source_target_pairs={{0,2},{1,3},{2,0},{3,1},{4,6},{5,7},{6,4},{7,5},{8,10},{9,11},{10,... | collective-permute-start | bytes 1032200 | tf_op jit(solution)/shard_map/ppermute | solution.py:29
  117.0 17.8 %collective-permute-start.33 = (bf16[64,2688]{1,0:T(8,128)(2,1)}, bf16[64,2688]{1,0:T(8,128)(2,1)S(1)}, u32[]{:S(2)}, u32[]{:S(2)}) collective-permute-start(bf16[64,2688]{1,0:T(8,128)(2,1)} %fusion.18), channel_id=1, source_target_pairs={{0,4},{1,5},{2,6},{3,7},{4,0},{5,1},{6,2},{7,3},{8,12},{9,13},{10,... | collective-permute-start | bytes 1032200 | tf_op jit(solution)/shard_map/ppermute | solution.py:29
  118.8 16.0 %collective-permute-start.31 = (bf16[64,2688]{1,0:T(8,128)(2,1)}, bf16[64,2688]{1,0:T(8,128)(2,1)S(1)}, u32[]{:S(2)}, u32[]{:S(2)}) collective-permute-start(bf16[64,2688]{1,0:T(8,128)(2,1)} %fusion.16), channel_id=1, source_target_pairs={{0,6},{1,7},{2,4},{3,5},{4,2},{5,3},{6,0},{7,1},{8,14},{9,15},{10,... | collective-permute-start | bytes 1032200 | tf_op jit(solution)/shard_map/ppermute | solution.py:29
  (6 other events, 150.6 us)

commit v3 on v2

v3 whole, which is shorter than its diff:
```python
import jax
import jax.numpy as jnp
from jax import lax
from jax.experimental import pallas as pl
from jax.experimental.pallas import tpu as pltpu
from jax.sharding import PartitionSpec as P


BF = jnp.bfloat16
F32 = jnp.float32
CORE, X, Y, Z = 1, 2, 4, 8
ROOM = {"head": 8, "main": 16, "far": 12, "near": 12, "bwd": 8, "join": 4, "again": 8}


def pick(bit, zero, one):
    return jnp.where(bit == 1, one, zero)


def arrange(pieces, bits):
    for k, bit in enumerate(bits):
        pieces = [pick(bit, pieces[i], pieces[i ^ (1 << k)]) for i in range(len(pieces))]
    return pieces


def nt_dot(a, b):
    return lax.dot_general(a, b, (((1,), (1,)), ((), ())), preferred_element_type=F32)


def tn_dot(a, b):
    return lax.dot_general(a, b, (((0,), (0,)), ((), ())), preferred_element_type=F32)


VM = pl.BlockSpec(memory_space=pltpu.VMEM)
SM = pl.BlockSpec(memory_space=pltpu.SMEM)


def local_call(kernel, shapes, scratch=(), flops=0, moved=0, smem=0, operands=(), room=16, keep=True):
    return pl.pallas_call(
        kernel,
        in_specs=[SM] * smem + [VM] * (len(operands) - smem),
        out_specs=[VM] * len(shapes),
        out_shape=[(pltpu.VMEM if keep else jax.ShapeDtypeStruct)(shape, dtype) for shape, dtype in shapes],
        scratch_shapes=list(scratch),
        cost_estimate=pl.CostEstimate(flops=flops, bytes_accessed=moved, transcendentals=0),
        compiler_params=pltpu.CompilerParams(vmem_limit_bytes=room << 20),
    )(*operands)


def join(parts, target):
    step = parts[0].shape[0]
    for i, part in enumerate(parts):
        target[i * step:(i + 1) * step, :] = part[...]


def cot_pass(place, cot):
    outs, rows = cot.shape
    blk = rows // 8

    def kernel(place_ref, cot_ref, cols_out, rows_out):
        here = place_ref[0]
        core, plane = here % 2, (here // 2) % 4
        for k in range(4):
            at = pl.multiple_of((4 * core + (plane ^ k)) * blk, blk)
            cols_out[:, k * blk:(k + 1) * blk] = cot_ref[:, pl.ds(at, blk)]
        shape = (outs, outs)
        same = lax.broadcasted_iota(jnp.int32, shape, 0) == lax.broadcasted_iota(jnp.int32, shape, 1)
        rows_out[...] = tn_dot(cols_out[...], jnp.where(same, 1.0, 0.0).astype(BF)).astype(BF)

    return local_call(
        kernel, [((outs, 4 * blk), BF), ((4 * blk, outs), BF)], smem=1, moved=4 * outs * rows,
        operands=(place, cot), room=4,
    )


def pred_step(place, parts, level):
    rows, outs = parts[0].shape
    half = rows // 2

    def kernel(place_ref, *refs):
        *ins, keep, sent, total = refs
        value = ins[0][...]
        for ref in ins[1:]:
            value = value + ref[...].astype(F32)
        total[...] = value
        bit = (place_ref[0] // (Z << level)) % 2
        keep[...] = total[pl.ds(pl.multiple_of(bit * half, half), half), :]
        sent[...] = total[pl.ds(pl.multiple_of((1 - bit) * half, half), half), :].astype(BF)

    return local_call(
        kernel, [((half, outs), F32), ((half, outs), BF)], [pltpu.VMEM((rows, outs), F32)],
        smem=1, moved=8 * rows * outs, operands=(place, *parts), room=2,
    )


def head_pass(place, weights, own, other, width, count):
    hid = weights[0].shape[0]
    pieces, rows = own.shape
    din, half, cols = 2 * pieces, rows // 2, 2 * pieces // count

    def kernel(place_ref, w0, w1, w2, w3, own_ref, other_ref, mine, theirs, emb_out, emb, first, second):
        here = place_ref[0]
        core, plane, depth = here % 2, (here // 2) % 4, here // Z
        for k in range(pieces // cols):
            source = (depth ^ (k // 4)) * Z + (plane ^ (k % 4)) * 2
            part = slice(k * cols, (k + 1) * cols)
            for ref, which in ((own_ref, core), (other_ref, 1 - core)):
                at = pl.multiple_of((source + which) * cols, cols)
                emb[pl.ds(at, cols), :] = ref[part, :]
        parts = (w0, w1, w2, w3)
        for i, part in enumerate(parts):
            first[i * hid:(i + 1) * hid, :] = part[:, :din]
            second[i * hid:(i + 1) * hid, :] = part[:, din:din + width]
        bias = jnp.concatenate(
            [jnp.sum(part[:, din + width:].astype(F32), axis=1, keepdims=True) for part in parts], axis=0
        )
        preact = jnp.dot(first[...], emb[...], preferred_element_type=F32) + bias
        hidden = jax.nn.gelu(preact).astype(BF)
        sums = tn_dot(hidden, second[...])

        @pl.when(core == 0)
        def _():
            mine[...] = sums[:half]
            theirs[...] = sums[half:]
            emb_out[...] = emb[:, :half]

        @pl.when(core == 1)
        def _():
            mine[...] = sums[half:]
            theirs[...] = sums[:half]
            emb_out[...] = emb[:, half:]

    return local_call(
        kernel, [((half, width), F32)] * 2 + [((din, half), BF)],
        [pltpu.VMEM((din, rows), BF), pltpu.VMEM((4 * hid, din), BF), pltpu.VMEM((4 * hid, width), BF)],
        flops=8 * hid * rows * (din + width), moved=8 * hid * din, smem=1,
        operands=(place, *weights, own, other), room=ROOM["head"],
    )


def point_pass(feats, cot, sets, norms, factor, tile=512):
    blk, width = feats[0].shape
    rows, points, outs = 4 * blk, sets[0][0].shape[0], cot.shape[1]
    tile = min(tile, points)
    scale = -8.0 / width

    def kernel(f0, f1, f2, f3, cot_ref, cen0, cen1, coef0, coef1, norm0, norm1,
               kern0, kern1, low0, low1, col0, col1, grad0, grad1, grad2, grad3, fs, acc):
        join((f0, f1, f2, f3), fs)
        wide = fs[...].astype(F32)
        feat_norm = scale * jnp.sum(wide * wide, axis=1, keepdims=True)
        acc[...] = jnp.zeros_like(acc)
        lanes = acc.shape[1]
        for cen, coef, norm, kern_out, low_out, col_out in (
            (cen0, coef0, norm0, kern0, low0, col0), (cen1, coef1, norm1, kern1, low1, col1)
        ):
            @pl.loop(0, points // tile)
            def _(i):
                at = pl.ds(pl.multiple_of(i * tile, tile), tile)
                inner = nt_dot(fs[...], cen[at, :])
                grad = jnp.dot(cot_ref[...], coef[:, at], preferred_element_type=F32)
                shift = feat_norm + scale * norm[:, at]
                kern = jnp.exp((-2.0 * scale) * inner + shift).astype(BF)
                weighted = grad * kern.astype(F32)
                kern_out[:, at] = kern
                low_out[:, at] = weighted.astype(BF)
                col_out[:, at] = jnp.sum(weighted, axis=0, keepdims=True)
                acc[...] += sum(weighted[:, k * lanes:(k + 1) * lanes] for k in range(tile // lanes))

        sums = jnp.sum(acc[...], axis=1, keepdims=True)
        grad = jnp.dot(low0[...], cen0[...], preferred_element_type=F32)
        grad = grad + jnp.dot(low1[...], cen1[...], preferred_element_type=F32)
        grad = -factor * (sums * fs[...].astype(F32) - grad)
        for k, out in enumerate((grad0, grad1, grad2, grad3)):
            out[...] = grad[k * blk:(k + 1) * blk].astype(out.dtype)

    return local_call(
        kernel,
        [((rows, points), BF)] * 4 + [((1, points), F32)] * 2 + [((blk, width), F32)] + [((blk, width), BF)] * 3,
        [pltpu.VMEM((rows, width), BF), pltpu.VMEM((rows, 128), F32)],
        flops=8 * rows * points * (width + outs), moved=16 * rows * points,
        operands=(*feats, cot, sets[0][0], sets[1][0], sets[0][1], sets[1][1], *norms), room=ROOM["main"],
    )


def far_points(feats, cot, kerns, lows, col, points_ref, coefs, factor, tile=512):
    blk, width = feats[0].shape
    rows, points, outs = 4 * blk, kerns[0].shape[1], cot.shape[0]
    tile = min(tile, points)

    def kernel(f0, f1, f2, f3, cot_ref, kern0, kern1, low, col_ref, cen, coef0, coef1, cen_out, coef_out, pred0, pred1, pred2, pred3, fs):
        join((f0, f1, f2, f3), fs)
        total = nt_dot(kern0[...], coef0[...]) + nt_dot(kern1[...], coef1[...])
        for k, out in enumerate((pred0, pred1, pred2, pred3)):
            out[...] = total[k * blk:(k + 1) * blk].astype(out.dtype)

        @pl.loop(0, points // tile)
        def _(i):
            at = pl.ds(pl.multiple_of(i * tile, tile), tile)
            sums = jnp.broadcast_to(col_ref[:, at], (128, tile)).T[:, :1]
            part = tn_dot(low[:, at], fs[...])
            cen_out[at, :] = (-factor * (sums * cen[at, :].astype(F32) - part)).astype(BF)
            coef_out[:, at] = jnp.dot(cot_ref[...], kern1[:, at], preferred_element_type=F32).astype(BF)

    return local_call(
        kernel, [((points, width), BF), ((outs, points), BF), ((blk, outs), F32)] + [((blk, outs), BF)] * 3,
        [pltpu.VMEM((rows, width), BF)],
        flops=2 * rows * points * (width + 3 * outs), moved=4 * rows * points,
        operands=(*feats, cot, *kerns, lows, col, points_ref, *coefs), room=ROOM["far"],
    )


def near_points(feats, cot, kern, low, col, points_ref, got_cen, got_coef, factor, tile=512):
    blk, width = feats[0].shape
    rows, points, outs = 4 * blk, kern.shape[1], cot.shape[0]
    tile = min(tile, points)

    def kernel(f0, f1, f2, f3, cot_ref, kern_ref, low_ref, col_ref, cen, got_c, got_k, cen_out, coef_out, fs):
        @pl.when(pl.program_id(0) == 0)
        def _():
            join((f0, f1, f2, f3), fs)

        at = pl.ds(pl.multiple_of(pl.program_id(0) * tile, tile), tile)
        sums = jnp.broadcast_to(col_ref[:, at], (128, tile)).T[:, :1]
        part = tn_dot(low_ref[:, at], fs[...])
        cen_out[...] = -factor * (sums * cen[at, :].astype(F32) - part) + got_c[at, :].astype(F32)
        coef_out[...] = (
            jnp.dot(cot_ref[...], kern_ref[:, at], preferred_element_type=F32) + got_k[:, at].astype(F32)
        )

    by_row = lambda n: pl.BlockSpec((tile, n), lambda i: (i, 0))
    by_col = lambda n: pl.BlockSpec((n, tile), lambda i: (0, i))
    return pl.pallas_call(
        kernel,
        grid=(points // tile,),
        in_specs=[VM] * 11,
        out_specs=[by_row(width), by_col(outs)],
        out_shape=[jax.ShapeDtypeStruct((points, width), F32), jax.ShapeDtypeStruct((outs, points), F32)],
        scratch_shapes=[pltpu.VMEM((rows, width), BF)],
        cost_estimate=pl.CostEstimate(
            flops=2 * rows * points * (width + outs), bytes_accessed=4 * rows * points, transcendentals=0
        ),
        compiler_params=pltpu.CompilerParams(vmem_limit_bytes=ROOM["near"] << 20),
    )(*feats, cot, kern, low, col, points_ref, got_cen, got_coef)


def head_again(own, other, embs, width):
    hid = own.shape[0]
    din, blk = embs[0].shape
    rows = 4 * blk

    def kernel(own_ref, other_ref, e0, e1, e2, e3, hidden_out, slope_out, second_out, emb_out, first):
        for k, ref in enumerate((e0, e1, e2, e3)):
            emb_out[:, k * blk:(k + 1) * blk] = ref[...]
        for k, ref in enumerate((own_ref, other_ref)):
            first[k * hid:(k + 1) * hid, :] = ref[:, :din]
            second_out[k * hid:(k + 1) * hid, :] = ref[:, din:din + width]
        bias = jnp.concatenate([
            jnp.sum(ref[:, din + width:].astype(F32), axis=1, keepdims=True) for ref in (own_ref, other_ref)
        ], axis=0)
        preact = jnp.dot(first[...], emb_out[...], preferred_element_type=F32) + bias
        hidden, pullback = jax.vjp(jax.nn.gelu, preact)
        hidden_out[...] = hidden.astype(BF)
        slope_out[...] = pullback(jnp.ones_like(preact))[0]

    return local_call(
        kernel,
        [((2 * hid, rows), BF), ((2 * hid, rows), F32), ((2 * hid, width), BF), ((din, rows), BF)],
        [pltpu.VMEM((2 * hid, din), BF)],
        flops=4 * hid * rows * din, moved=4 * rows * din,
        operands=(own, other, *embs), room=ROOM["again"],
    )


def head_grads(phis, hidden, slope, second, emb):
    _, width = phis[0].shape
    din, rows = emb.shape
    hid = hidden.shape[0] // 2

    def kernel(p0, p1, p2, p3, hid_ref, slope_ref, w_ref, emb_ref, first_out, second_out, bias_out, sent, phi):
        join((p0, p1, p2, p3), phi)
        grad = nt_dot(w_ref[...], phi[...]) * slope_ref[...]
        low = grad.astype(BF)
        rest = (grad - low.astype(F32)).astype(BF)
        ones = jnp.ones((16, rows), BF)
        firsts = nt_dot(low, emb_ref[...])
        seconds = jnp.dot(hid_ref[...], phi[...], preferred_element_type=F32)
        first_out[...] = firsts[:hid]
        second_out[...] = seconds[:hid]
        bias_out[...] = nt_dot(ones, low[:hid]) + nt_dot(ones, rest[:hid])
        sent[:hid, :din] = firsts[hid:].astype(BF)
        sent[:hid, din:] = seconds[hid:].astype(BF)
        sent[hid:, :] = jnp.zeros((16, din + width), BF)
        sent[hid:, :hid] = (nt_dot(ones, low[hid:]) + nt_dot(ones, rest[hid:])).astype(BF)

    return local_call(
        kernel,
        [((hid, din), F32), ((hid, width), F32), ((16, hid), F32), ((hid + 16, din + width), BF)],
        [pltpu.VMEM((rows, width), BF)],
        flops=4 * hid * rows * (din + 2 * width), moved=4 * rows * din,
        operands=(*phis, hidden, slope, second, emb), room=ROOM["bwd"],
    )


def head_join(first, second, bias, got):
    hid, din = first.shape

    def kernel(first_ref, second_ref, bias_ref, got_ref, first_out, second_out, bias_out):
        first_out[...] = first_ref[...] + got_ref[:hid, :din].astype(F32)
        second_out[...] = second_ref[...] + got_ref[:hid, din:].astype(F32)
        bias_out[...] = bias_ref[:1, :] + got_ref[hid:, :hid][:1, :].astype(F32)

    return local_call(
        kernel, [(first.shape, F32), (second.shape, F32), ((1, hid), F32)],
        moved=12 * hid * din, operands=(first, second, bias, got), room=ROOM["join"], keep=False,
    )


def make_body(count, groups):
    deep = count // Z
    levels = deep.bit_length() - 1

    def send(value, pairs):
        return lax.ppermute(value, "center", pairs)

    def swap(value, bit):
        return send(value, [(i, i ^ bit) for i in range(count)])

    def owner(i):
        block = (i & 1) * 4 + ((i >> 1) & 3)
        return deep * block + i // Z

    def inner_body(embeddings, first_weight, first_bias, second_weight, centers, coefficients, cotangent):
        feat_width = centers.shape[1]
        factor = 16.0 / feat_width
        rows = embeddings.shape[0]
        blk = rows // 8
        _, hid = first_weight.shape
        place = lax.axis_index("center")
        xbit, ybit = (place >> 1) & 1, (place >> 2) & 1
        plane = [xbit, ybit]

        local = embeddings.T
        slabs = [
            jnp.concatenate([local[:, (4 * c + p) * blk:][:, :blk] for c in range(2)], axis=1)
            for p in range(4)
        ]
        slabs = arrange(slabs, plane)
        got = {k: swap(slabs[k], k * X) for k in (3, 1, 2)}
        block = jnp.concatenate([slabs[0], got[1], got[2], got[3]], axis=0)

        high = first_bias.astype(BF)
        low = (first_bias - high.astype(F32)).astype(BF)
        spread = jnp.concatenate([high, low])
        hids = lax.broadcasted_iota(jnp.int32, (hid, 2 * hid), 0)
        slots = lax.broadcasted_iota(jnp.int32, (hid, 2 * hid), 1) % hid
        bias_cols = jnp.where(hids == slots, spread[None, :], jnp.zeros((), BF))
        bias_cols = jnp.pad(bias_cols, ((0, 0), (0, -2 * hid % 128)))
        own_weights = jnp.concatenate([first_weight.T, second_weight, bias_cols], axis=1)
        got = {k: swap(own_weights, k * X) for k in (3, 1, 2)}
        weights = [own_weights, got[1], got[2], got[3]]
        core_weights = swap(own_weights, CORE)

        block = jnp.concatenate([block] + [swap(block, k * Z) for k in range(1, deep)], axis=0)
        other = swap(block, CORE)
        mine, theirs, emb_own = head_pass(place[None], weights, block, other, feat_width, count)
        total = mine + swap(theirs, CORE)

        def deep_sum(value):
            for k in range(levels):
                low_value = value.astype(BF)
                value = low_value.astype(F32) + swap(low_value, Z << k).astype(F32)
            return value

        feature_sum = deep_sum(total)
        squashed = jnp.tanh(feature_sum)
        own_feats = squashed.astype(BF)
        got = {k: swap(own_feats, k * X) for k in (3, 1, 2)}

        cot, cot_rows = cot_pass(place[None], cotangent.T)

        emb_x, emb_y = swap(emb_own, X), swap(emb_own, Y)
        emb_xy = swap(emb_y, X)

        coef_own = coefficients.T
        sets = [
            (centers, coef_own),
            (swap(centers, CORE), swap(coef_own, CORE)),
        ]
        norms = []
        for points, coef in sets:
            wide = points.astype(F32)
            norms.append(jnp.sum(wide * wide, axis=1)[None, :])
        feats = [own_feats, got[1], got[2], got[3]]
        kern0, kern1, low0, low1, col0, col1, *grads = point_pass(feats, cot_rows, sets, norms, factor)

        def plane_sum(parts):
            got = [swap(parts[k], k * X) for k in (3, 1, 2)]
            return parts[0].astype(F32) + sum(part.astype(F32) for part in got)

        feature_grad = deep_sum(plane_sum(grads))
        phi_own = (feature_grad * (1.0 - squashed * squashed)).astype(BF)
        got = {k: swap(phi_own, k * X) for k in (3, 1, 2)}
        phis = [phi_own, got[1], got[2], got[3]]

        far_cen, far_coef, *preds = far_points(
            feats, cot, (kern0, kern1), low1, col1, sets[1][0], (sets[0][1], sets[1][1]), factor
        )
        got = {k: swap(preds[k], k * X) for k in (3, 1, 2)}
        parts = [preds[0], got[1], got[2], got[3]]
        for k in reversed(range(levels)):
            keep, sent = pred_step(place[None], parts, k)
            parts = [keep, swap(sent, Z << k)]
        preds = sum(part.astype(F32) for part in parts)
        predictions = send(preds.astype(BF), [(i, owner(i)) for i in range(count)]).astype(F32)

        got_cen, got_coef = swap(far_cen, CORE), swap(far_coef, CORE)
        center_grad, coef_grad = near_points(
            feats, cot, kern0, low0, col0, centers, got_cen, got_coef, factor
        )
        coef_grad = coef_grad.T

        hidden, slope, second, emb_rows = head_again(
            own_weights, core_weights, [emb_own, emb_x, emb_y, emb_xy], feat_width
        )
        first_grad, second_grad, bias_grad, sent = head_grads(phis, hidden, slope, second, emb_rows)
        got = swap(sent, CORE)
        first_grad, second_grad, bias_grad = head_join(first_grad, second_grad, bias_grad, got)
        first_grad = first_grad.T
        bias_grad = bias_grad[0]
        if groups > 1:
            first_grad, second_grad, center_grad = (
                lax.psum_scatter(first_grad.astype(BF), "dp", scatter_dimension=0, tiled=True).astype(F32),
                lax.psum_scatter(second_grad.astype(BF), "dp", scatter_dimension=1, tiled=True).astype(F32),
                lax.psum_scatter(center_grad.astype(BF), "dp", scatter_dimension=1, tiled=True).astype(F32),
            )
            bias_grad, coef_grad = (
                lax.psum(bias_grad.astype(BF), "dp").astype(F32),
                lax.psum(coef_grad.astype(BF), "dp").astype(F32),
            )
        return (predictions, first_grad, bias_grad, second_grad, center_grad, coef_grad)

    return inner_body


def solution(mesh):
    placed = (
        P("dp", "center"),
        P(None, "center"),
        P("center"),
        P("center", None),
        P("center", None),
        P("center", None),
        P("dp", None),
    )
    count, groups = mesh.shape["center"], mesh.shape["dp"]
    return jax.shard_map(
        make_body(count, groups),
        mesh=mesh,
        in_specs=placed,
        out_specs=(
            P(("dp", "center"), None),
            P("dp", "center"),
            P("center"),
            P("center", "dp"),
            P("center", "dp"),
            P("center", None),
        ),
        check_vma=False,
    )
```

time: 137 us -> 162 us (1.18)
  the two profiles are of different devices: /device:TPU:0 before, /device:TPU:20 now
where the time goes in v3:
time: 162 us
  waiting for transfers between devices  98.6 us (61%)
  starting transfers between devices  37.7 us (23%)
  Pallas kernels  20.3 us (13%)
  other arithmetic  3.79 us (2%)
    ppermute x39, waiting for transfers between devices, send(): return lax.ppermute(value, 'center', pairs)  98.6 us
    ppermute x39, starting transfers between devices, send(): return lax.ppermute(value, 'center', pairs)  37.7 us
    pallas_call x9, Pallas kernels, local_call(): pl.pallas_call(kernel, in_specs=[SM] * smem + [VM] * (len(operands) - sme...  16.4 us
    pallas_call x1, Pallas kernels, near_points(): pl.pallas_call(kernel, grid=(points // tile,), in_specs=[VM] * 11, out_sp...  3.85 us
  transfers between devices with their start and end apart: 39, of which 27 were waited for; matrix products, arithmetic and copies ran while one was open for 2% of the time, Pallas kernels for 3%

profile of v3, /device:TPU:20, one launch (start us, length us, event | category | flops | bytes accessed | tf_op | source)
XLA Modules:
  0.0 162.2 jit_solution(1840031466551825455)
XLA Ops:
  2.2 1.6 collective-permute-start.3
  6.2 2.4 %collective-permute-done.5 = bf16[64,256]{1,0:T(8,128)(2,1)S(1)} collective-permute-done((bf16[64,256]{1,0:T(8,128)(2,1)S(1)}, bf16[64,256]{1,0:T(8,128)(2,1)S(1)}, u32[]{:S(2)}, u32[]{:S(2)}) %collective-permute-start.5) | collective-permute-done | bytes 32800 | tf_op jit(solution)/shard_map/ppermute | solution.py:323
  8.6 1.6 %collective-permute-start.6 = (bf16[256,256]{1,0:T(8,128)(2,1)S(1)}, bf16[256,256]{1,0:T(8,128)(2,1)S(1)}, u32[]{:S(2)}, u32[]{:S(2)}) collective-permute-start(bf16[256,256]{1,0:T(8,128)(2,1)S(1)} %pad_maximum_fusion.1), channel_id=1, source_target_pairs={{0,8},{1,9},{2,10},{3,11},{4,12},{5,13},{6,14},{7,15},{8,0},{9,1},... | collective-permute-start | bytes 393224 | tf_op jit(solution)/shard_map/ppermute | solution.py:323
  10.5 1.6 collective-permute-start.8
  12.1 2.4 %collective-permute-done.6 = bf16[256,256]{1,0:T(8,128)(2,1)S(1)} collective-permute-done((bf16[256,256]{1,0:T(8,128)(2,1)S(1)}, bf16[256,256]{1,0:T(8,128)(2,1)S(1)}, u32[]{:S(2)}, u32[]{:S(2)}) %collective-permute-start.6) | collective-permute-done | bytes 131104 | tf_op jit(solution)/shard_map/ppermute | solution.py:323
  14.6 3.8 %collective-permute-done.7 = bf16[256,256]{1,0:T(8,128)(2,1)S(1)} collective-permute-done((bf16[256,256]{1,0:T(8,128)(2,1)S(1)}, bf16[256,256]{1,0:T(8,128)(2,1)S(1)}, u32[]{:S(2)}, u32[]{:S(2)}) %collective-permute-start.7) | collective-permute-done | bytes 131104 | tf_op jit(solution)/shard_map/ppermute | solution.py:323
  18.4 3.5 %collective-permute-done.8 = bf16[256,256]{1,0:T(8,128)(2,1)S(1)} collective-permute-done((bf16[256,256]{1,0:T(8,128)(2,1)S(1)}, bf16[256,256]{1,0:T(8,128)(2,1)S(1)}, u32[]{:S(2)}, u32[]{:S(2)}) %collective-permute-start.8) | collective-permute-done | bytes 131104 | tf_op jit(solution)/shard_map/ppermute | solution.py:323
  26.6 7.4 %collective-permute-done.w1 = bf16[64,2688]{1,0:T(8,128)(2,1)S(1)} collective-permute-done((bf16[64,2688]{1,0:T(8,128)(2,1)S(1)}, bf16[64,2688]{1,0:T(8,128)(2,1)S(1)}, u32[]{:S(2)}, u32[]{:S(2)}) %collective-permute-start) | collective-permute-done | bytes 344096 | tf_op jit(solution)/shard_map/ppermute | solution.py:323
  34.0 7.9 %collective-permute-done.1.w2 = bf16[64,2688]{1,0:T(8,128)(2,1)S(1)} collective-permute-done((bf16[64,2688]{1,0:T(8,128)(2,1)S(1)}, bf16[64,2688]{1,0:T(8,128)(2,1)S(1)}, u32[]{:S(2)}, u32[]{:S(2)}) %collective-permute-start.1) | collective-permute-done | bytes 344096 | tf_op jit(solution)/shard_map/ppermute | solution.py:323
  43.1 1.5 collective-permute-done.10
  45.2 5.0 %collective-permute-done.11 = bf16[128,512]{1,0:T(8,128)(2,1)S(1)} collective-permute-done((bf16[128,512]{1,0:T(8,128)(2,1)S(1)}, bf16[128,512]{1,0:T(8,128)(2,1)S(1)}, u32[]{:S(2)}, u32[]{:S(2)}) %collective-permute-start.11) | collective-permute-done | bytes 131104 | tf_op jit(solution)/shard_map/ppermute | solution.py:323
  51.0 5.2 %collective-permute-done.12 = bf16[128,512]{1,0:T(8,128)(2,1)S(1)} collective-permute-done((bf16[128,512]{1,0:T(8,128)(2,1)S(1)}, bf16[128,512]{1,0:T(8,128)(2,1)S(1)}, u32[]{:S(2)}, u32[]{:S(2)}) %collective-permute-start.12) | collective-permute-done | bytes 131104 | tf_op jit(solution)/shard_map/ppermute | solution.py:323
  62.8 1.5 collective-permute-done.15.f3
  64.3 8.6 %shard_map.120 = (bf16[512,2048]{1,0:T(8,128)(2,1)S(1)}, bf16[512,2048]{1,0:T(8,128)(2,1)S(1)}, bf16[512,2048]{1,0:T(8,128)(2,1)S(1)}, bf16[512,2048]{1,0:T(8,12...) custom-call(bf16[128,512]{1,0:T(8,128)(2,1)S(1)} %fusion.f0, ...), custom_call_target="tpu_custom_call" | custom-call | flops 5133828096 | bytes 16777216 | tf_op jit(solution)/shard_map/pallas_call | solution.py:38
  72.9 3.5 %shard_map.121 = (bf16[2048,512]{1,0:T(8,128)(2,1)S(1)}, bf16[100,2048]{1,0:T(8,128)(2,1)S(1)}, f32[128,100]{1,0:T(8,128)S(1)}, bf16[128,100]{1,0:T(8,128)(2,1)S...) custom-call(bf16[128,512]{1,0:T(8,128)(2,1)S(1)} %fusion.f0, ...), custom_call_target="tpu_custom_call" | custom-call | flops 1702887424 | bytes 4194304 | tf_op jit(solution)/shard_map/pallas_call | solution.py:38
  80.7 3.8 %collective-permute-done.24 = bf16[128,512]{1,0:T(8,128)(2,1)S(1)} collective-permute-done((bf16[128,512]{1,0:T(8,128)(2,1)S(1)}, bf16[128,512]{1,0:T(8,128)(2,1)S(1)}, u32[]{:S(2)}, u32[]{:S(2)}) %collective-permute-start.24) | collective-permute-done | bytes 131104 | tf_op jit(solution)/shard_map/ppermute | solution.py:323
  84.5 1.9 %collective-permute-done.25 = bf16[128,512]{1,0:T(8,128)(2,1)S(1)} collective-permute-done((bf16[128,512]{1,0:T(8,128)(2,1)S(1)}, bf16[128,512]{1,0:T(8,128)(2,1)S(1)}, u32[]{:S(2)}, u32[]{:S(2)}) %collective-permute-start.25) | collective-permute-done | bytes 131104 | tf_op jit(solution)/shard_map/ppermute | solution.py:323
  86.5 10.0 %collective-permute-done.26 = bf16[128,512]{1,0:T(8,128)(2,1)S(1)} collective-permute-done((bf16[128,512]{1,0:T(8,128)(2,1)S(1)}, bf16[128,512]{1,0:T(8,128)(2,1)S(1)}, u32[]{:S(2)}, u32[]{:S(2)}) %collective-permute-start.26) | collective-permute-done | bytes 131104 | tf_op jit(solution)/shard_map/ppermute | solution.py:323
  96.5 3.5 %collective-permute-start.27 = (bf16[128,512]{1,0:T(8,128)(2,1)S(1)}, bf16[128,512]{1,0:T(8,128)(2,1)S(1)}, u32[]{:S(2)}, u32[]{:S(2)}) collective-permute-start(bf16[128,512]{1,0:T(8,128)(2,1)S(1)} %add_convert_fusion.1), channel_id=1, source_target_pairs={{0,8},{1,9},{2,10},{3,11},{4,12},{5,13},{6,14},{7,15},{8,0},{9,1},... | collective-permute-start | bytes 393224 | tf_op jit(solution)/shard_map/ppermute | solution.py:323
  103.3 1.6 %collective-permute-start.28 = (bf16[128,512]{1,0:T(8,128)(2,1)S(1)}, bf16[128,512]{1,0:T(8,128)(2,1)S(1)}, u32[]{:S(2)}, u32[]{:S(2)}) collective-permute-start(bf16[128,512]{1,0:T(8,128)(2,1)S(1)} %add_convert_fusion), channel_id=1, source_target_pairs={{0,16},{1,17},{2,18},{3,19},{4,20},{5,21},{6,22},{7,23},{8,24},{9,... | collective-permute-start | bytes 393224 | tf_op jit(solution)/shard_map/ppermute | solution.py:323
  104.9 4.4 %collective-permute-done.28 = bf16[128,512]{1,0:T(8,128)(2,1)S(1)} collective-permute-done((bf16[128,512]{1,0:T(8,128)(2,1)S(1)}, bf16[128,512]{1,0:T(8,128)(2,1)S(1)}, u32[]{:S(2)}, u32[]{:S(2)}) %collective-permute-start.28) | collective-permute-done | bytes 131104 | tf_op jit(solution)/shard_map/ppermute | solution.py:323
  111.6 3.2 %collective-permute-done.33.e1 = bf16[2048,128]{1,0:T(8,128)(2,1)S(1)} collective-permute-done((bf16[2048,128]{1,0:T(8,128)(2,1)S(1)}, bf16[2048,128]{1,0:T(8,128)(2,1)S(1)}, u32[]{:S(2)}, u32[]{:S(2)}) %collective-permute-start.33) | collective-permute-done | bytes 524320 | tf_op jit(solution)/shard_map/ppermute | solution.py:323
  116.3 9.8 %collective-permute-done.35.e3 = bf16[2048,128]{1,0:T(8,128)(2,1)S(1)} collective-permute-done((bf16[2048,128]{1,0:T(8,128)(2,1)S(1)}, bf16[2048,128]{1,0:T(8,128)(2,1)S(1)}, u32[]{:S(2)}, u32[]{:S(2)}) %collective-permute-start.35) | collective-permute-done | bytes 524320 | tf_op jit(solution)/shard_map/ppermute | solution.py:323
  127.0 1.6 collective-permute-done.29.p1
  128.6 1.7 %collective-permute-done.31.p3 = bf16[128,512]{1,0:T(8,128)(2,1)S(1)} collective-permute-done((bf16[128,512]{1,0:T(8,128)(2,1)S(1)}, bf16[128,512]{1,0:T(8,128)(2,1)S(1)}, u32[]{:S(2)}, u32[]{:S(2)}) %collective-permute-start.31) | collective-permute-done | bytes 131104 | tf_op jit(solution)/shard_map/ppermute | solution.py:323
  134.0 1.9 %collective-permute-done.18.refs_1_ = bf16[128,100]{1,0:T(8,128)(2,1)S(1)} collective-permute-done((bf16[128,100]{1,0:T(8,128)(2,1)S(1)}, bf16[128,100]{1,0:T(8,128)(2,1)S(1)}, u32[]{:S(2)}, u32[]{:S(2)}) %collective-permute-start.18) | collective-permute-done | bytes 25632 | tf_op jit(solution)/shard_map/ppermute | solution.py:323
  137.3 3.4 %collective-permute-done.20.refs_3_ = bf16[128,100]{1,0:T(8,128)(2,1)S(1)} collective-permute-done((bf16[128,100]{1,0:T(8,128)(2,1)S(1)}, bf16[128,100]{1,0:T(8,128)(2,1)S(1)}, u32[]{:S(2)}, u32[]{:S(2)}) %collective-permute-start.20) | collective-permute-done | bytes 25632 | tf_op jit(solution)/shard_map/ppermute | solution.py:323
  140.9 4.5 %collective-permute-done.21.refs_1_ = bf16[64,100]{1,0:T(8,128)(2,1)S(1)} collective-permute-done((bf16[64,100]{1,0:T(8,128)(2,1)S(1)}, bf16[64,100]{1,0:T(8,128)(2,1)S(1)}, u32[]{:S(2)}, u32[]{:S(2)}) %collective-permute-start.21) | collective-permute-done | bytes 12832 | tf_op jit(solution)/shard_map/ppermute | solution.py:323
  145.8 3.3 %collective-permute-done.22 = bf16[32,100]{1,0:T(8,128)(2,1)S(1)} collective-permute-done((bf16[32,100]{1,0:T(8,128)(2,1)S(1)}, bf16[32,100]{1,0:T(8,128)(2,1)S(1)}, u32[]{:S(2)}, u32[]{:S(2)}) %collective-permute-start.22) | collective-permute-done | bytes 6432 | tf_op jit(solution)/shard_map/ppermute | solution.py:323
  149.1 3.2 %collective-permute-start.23 = (bf16[32,100]{1,0:T(8,128)(2,1)S(1)}, bf16[32,100]{1,0:T(8,128)(2,1)S(1)}, u32[]{:S(2)}, u32[]{:S(2)}) collective-permute-start(bf16[32,100]{1,0:T(8,128)(2,1)S(1)} %add_convert_fusion.4), channel_id=1, source_target_pairs={{0,0},{1,16},{2,4},{3,20},{4,8},{5,24},{6,12},{7,28},{8,1},{9,17},... | collective-permute-start | bytes 19208 | tf_op jit(solution)/shard_map/ppermute | solution.py:323
  152.4 4.4 %collective-permute-done.23 = bf16[32,100]{1,0:T(8,128)(2,1)S(1)} collective-permute-done((bf16[32,100]{1,0:T(8,128)(2,1)S(1)}, bf16[32,100]{1,0:T(8,128)(2,1)S(1)}, u32[]{:S(2)}, u32[]{:S(2)}) %collective-permute-start.23) | collective-permute-done | bytes 6432 | tf_op jit(solution)/shard_map/ppermute | solution.py:323
  158.3 3.9 %shard_map.127 = (f32[2048,512]{1,0:T(8,128)}, f32[100,2048]{1,0:T(8,128)}) custom-call(bf16[128,512]{1,0:T(8,128)(2,1)S(1)} %fusion.f0, bf16[128,512]{1,0:T(8,128)(2,1)S(1)} %collective-permute-done.13.f1, bf16[128,512]{1,0:T(8,128)(2,1)S(1)} %collective-permute-done.14.f2, bf16[128,512]{1,0:T(8,128)(2,1)S(1)} %collective-permute-done.15.f3, ...), custom_call_target="tpu_custom_call" | custom-call | flops 1283457024 | bytes 4194304 | tf_op jit(solution)/shard_map/pallas_call | solution.py:232
  (90 shorter events, 37.5 us)
Async XLA Ops:
  3.7 4.8 %collective-permute-start.5 = (bf16[64,256]{1,0:T(8,128)(2,1)S(1)}, bf16[64,256]{1,0:T(8,128)(2,1)S(1)}, u32[]{:S(2)}, u32[]{:S(2)}) collective-permute-start(bf16[64,256]{1,0:T(8,128)(2,1)S(1)} %get-tuple-element.84), channel_id=1, source_target_pairs={{0,6},{1,7},{2,4},{3,5},{4,2},{5,3},{6,0},{7,1},{8,14},{9,15},{10,... | collective-permute-start | bytes 98312 | tf_op jit(solution)/shard_map/ppermute | solution.py:323
  5.2 54.6 %collective-permute-start.16 = (bf16[2048,512]{1,0:T(8,128)(2,1)}, bf16[2048,512]{1,0:T(8,128)(2,1)S(1)}, u32[]{:S(2)}, u32[]{:S(2)}) collective-permute-start(bf16[2048,512]{1,0:T(8,128)(2,1)} %cen.1), channel_id=1, source_target_pairs={{0,1},{1,0},{2,3},{3,2},{4,5},{5,4},{6,7},{7,6},{8,9},{9,8},{10,11... | collective-permute-start | bytes 6291464 | tf_op jit(solution)/shard_map/ppermute | solution.py:323
  8.6 6.0 %collective-permute-start.6 = (bf16[256,256]{1,0:T(8,128)(2,1)S(1)}, bf16[256,256]{1,0:T(8,128)(2,1)S(1)}, u32[]{:S(2)}, u32[]{:S(2)}) collective-permute-start(bf16[256,256]{1,0:T(8,128)(2,1)S(1)} %pad_maximum_fusion.1), channel_id=1, source_target_pairs={{0,8},{1,9},{2,10},{3,11},{4,12},{5,13},{6,14},{7,15},{8,0},{9,1},... | collective-permute-start | bytes 393224 | tf_op jit(solution)/shard_map/ppermute | solution.py:323
  10.2 8.2 %collective-permute-start.7 = (bf16[256,256]{1,0:T(8,128)(2,1)S(1)}, bf16[256,256]{1,0:T(8,128)(2,1)S(1)}, u32[]{:S(2)}, u32[]{:S(2)}) collective-permute-start(bf16[256,256]{1,0:T(8,128)(2,1)S(1)} %pad_maximum_fusion.1), channel_id=1, source_target_pairs={{0,16},{1,17},{2,18},{3,19},{4,20},{5,21},{6,22},{7,23},{8,24},{9,... | collective-permute-start | bytes 393224 | tf_op jit(solution)/shard_map/ppermute | solution.py:323
  10.5 11.4 %collective-permute-start.8 = (bf16[256,256]{1,0:T(8,128)(2,1)S(1)}, bf16[256,256]{1,0:T(8,128)(2,1)S(1)}, u32[]{:S(2)}, u32[]{:S(2)}) collective-permute-start(bf16[256,256]{1,0:T(8,128)(2,1)S(1)} %pad_maximum_fusion.1), channel_id=1, source_target_pairs={{0,24},{1,25},{2,26},{3,27},{4,28},{5,29},{6,30},{7,31},{8,16},{9,... | collective-permute-start | bytes 393224 | tf_op jit(solution)/shard_map/ppermute | solution.py:323
  21.9 20.1 %collective-permute-start.9 = (bf16[1024,256]{1,0:T(8,128)(2,1)S(1)}, bf16[1024,256]{1,0:T(8,128)(2,1)S(1)}, u32[]{:S(2)}, u32[]{:S(2)}) collective-permute-start(bf16[1024,256]{1,0:T(8,128)(2,1)S(1)} %constant_dynamic-update-slice_fusion.own_ref), channel_id=1, source_target_pairs={{0,1},{1,0},{2,3},{3,2},{4,5},{5,4},{6,7},{7,6},{8,9},{9,8},{10,11... | collective-permute-start | bytes 1572872 | tf_op jit(solution)/shard_map/ppermute | solution.py:323
  23.0 11.0 %collective-permute-start = (bf16[64,2688]{1,0:T(8,128)(2,1)S(1)}, bf16[64,2688]{1,0:T(8,128)(2,1)S(1)}, u32[]{:S(2)}, u32[]{:S(2)}) collective-permute-start(bf16[64,2688]{1,0:T(8,128)(2,1)S(1)} %pad_maximum_fusion.w0.own_ref), channel_id=1, source_target_pairs={{0,2},{1,3},{2,0},{3,1},{4,6},{5,7},{6,4},{7,5},{8,10},{9,11},{10,... | collective-permute-start | bytes 1032200 | tf_op jit(solution)/shard_map/ppermute | solution.py:323
  24.4 17.5 %collective-permute-start.1 = (bf16[64,2688]{1,0:T(8,128)(2,1)S(1)}, bf16[64,2688]{1,0:T(8,128)(2,1)S(1)}, u32[]{:S(2)}, u32[]{:S(2)}) collective-permute-start(bf16[64,2688]{1,0:T(8,128)(2,1)S(1)} %pad_maximum_fusion.w0.own_ref), channel_id=1, source_target_pairs={{0,4},{1,5},{2,6},{3,7},{4,0},{5,1},{6,2},{7,3},{8,12},{9,13},{10,... | collective-permute-start | bytes 1032200 | tf_op jit(solution)/shard_map/ppermute | solution.py:323
  25.2 16.8 %collective-permute-start.2 = (bf16[64,2688]{1,0:T(8,128)(2,1)S(1)}, bf16[64,2688]{1,0:T(8,128)(2,1)S(1)}, u32[]{:S(2)}, u32[]{:S(2)}) collective-permute-start(bf16[64,2688]{1,0:T(8,128)(2,1)S(1)} %pad_maximum_fusion.w0.own_ref), channel_id=1, source_target_pairs={{0,6},{1,7},{2,4},{3,5},{4,2},{5,3},{6,0},{7,1},{8,14},{9,15},{10,... | collective-permute-start | bytes 1032200 | tf_op jit(solution)/shard_map/ppermute | solution.py:323
  44.6 5.6 %collective-permute-start.11 = (bf16[128,512]{1,0:T(8,128)(2,1)S(1)}, bf16[128,512]{1,0:T(8,128)(2,1)S(1)}, u32[]{:S(2)}, u32[]{:S(2)}) collective-permute-start(bf16[128,512]{1,0:T(8,128)(2,1)S(1)} %add_convert_fusion.3), channel_id=1, source_target_pairs={{0,8},{1,9},{2,10},{3,11},{4,12},{5,13},{6,14},{7,15},{8,0},{9,1},... | collective-permute-start | bytes 393224 | tf_op jit(solution)/shard_map/ppermute | solution.py:323
  44.8 15.5 %collective-permute-start.17 = (bf16[100,2048]{1,0:T(8,128)(2,1)S(1)}, bf16[100,2048]{1,0:T(8,128)(2,1)S(1)}, u32[]{:S(2)}, u32[]{:S(2)}) collective-permute-start(bf16[100,2048]{1,0:T(8,128)(2,1)S(1)} %bitcast.10), channel_id=1, source_target_pairs={{0,1},{1,0},{2,3},{3,2},{4,5},{5,4},{6,7},{7,6},{8,9},{9,8},{10,11... | collective-permute-start | bytes 1228808 | tf_op jit(solution)/shard_map/ppermute | solution.py:323
  50.3 5.9 %collective-permute-start.12 = (bf16[128,512]{1,0:T(8,128)(2,1)S(1)}, bf16[128,512]{1,0:T(8,128)(2,1)S(1)}, u32[]{:S(2)}, u32[]{:S(2)}) collective-permute-start(bf16[128,512]{1,0:T(8,128)(2,1)S(1)} %add_convert_fusion.2), channel_id=1, source_target_pairs={{0,16},{1,17},{2,18},{3,19},{4,20},{5,21},{6,22},{7,23},{8,24},{9,... | collective-permute-start | bytes 393224 | tf_op jit(solution)/shard_map/ppermute | solution.py:323
  56.3 5.5 %collective-permute-start.13 = (bf16[128,512]{1,0:T(8,128)(2,1)S(1)}, bf16[128,512]{1,0:T(8,128)(2,1)S(1)}, u32[]{:S(2)}, u32[]{:S(2)}) collective-permute-start(bf16[128,512]{1,0:T(8,128)(2,1)S(1)} %fusion.f0), channel_id=1, source_target_pairs={{0,2},{1,3},{2,0},{3,1},{4,6},{5,7},{6,4},{7,5},{8,10},{9,11},{10,... | collective-permute-start | bytes 393224 | tf_op jit(solution)/shard_map/ppermute | solution.py:323
  57.0 5.8 %collective-permute-start.14 = (bf16[128,512]{1,0:T(8,128)(2,1)S(1)}, bf16[128,512]{1,0:T(8,128)(2,1)S(1)}, u32[]{:S(2)}, u32[]{:S(2)}) collective-permute-start(bf16[128,512]{1,0:T(8,128)(2,1)S(1)} %fusion.f0), channel_id=1, source_target_pairs={{0,4},{1,5},{2,6},{3,7},{4,0},{5,1},{6,2},{7,3},{8,12},{9,13},{10,... | collective-permute-start | bytes 393224 | tf_op jit(solution)/shard_map/ppermute | solution.py:323
  58.4 5.9 %collective-permute-start.15 = (bf16[128,512]{1,0:T(8,128)(2,1)S(1)}, bf16[128,512]{1,0:T(8,128)(2,1)S(1)}, u32[]{:S(2)}, u32[]{:S(2)}) collective-permute-start(bf16[128,512]{1,0:T(8,128)(2,1)S(1)} %fusion.f0), channel_id=1, source_target_pairs={{0,6},{1,7},{2,4},{3,5},{4,2},{5,3},{6,0},{7,1},{8,14},{9,15},{10,... | collective-permute-start | bytes 393224 | tf_op jit(solution)/shard_map/ppermute | solution.py:323
  76.4 81.9 %collective-permute-start.37 = (bf16[2048,512]{1,0:T(8,128)(2,1)S(1)}, bf16[2048,512]{1,0:T(8,128)(2,1)S(1)}, u32[]{:S(2)}, u32[]{:S(2)}) collective-permute-start(bf16[2048,512]{1,0:T(8,128)(2,1)S(1)} %get-tuple-element.78), channel_id=1, source_target_pairs={{0,1},{1,0},{2,3},{3,2},{4,5},{5,4},{6,7},{7,6},{8,9},{9,8},{10,11... | collective-permute-start | bytes 6291464 | tf_op jit(solution)/shard_map/ppermute | solution.py:323
  76.5 24.3 %collective-permute-start.34 = (bf16[2048,128]{1,0:T(8,128)(2,1)S(1)}, bf16[2048,128]{1,0:T(8,128)(2,1)S(1)}, u32[]{:S(2)}, u32[]{:S(2)}) collective-permute-start(bf16[2048,128]{1,0:T(8,128)(2,1)S(1)} %get-tuple-element.64.e0), channel_id=1, source_target_pairs={{0,4},{1,5},{2,6},{3,7},{4,0},{5,1},{6,2},{7,3},{8,12},{9,13},{10,... | collective-permute-start | bytes 1572872 | tf_op jit(solution)/shard_map/ppermute | solution.py:323
  77.2 7.3 %collective-permute-start.24 = (bf16[128,512]{1,0:T(8,128)(2,1)S(1)}, bf16[128,512]{1,0:T(8,128)(2,1)S(1)}, u32[]{:S(2)}, u32[]{:S(2)}) collective-permute-start(bf16[128,512]{1,0:T(8,128)(2,1)S(1)} %get-tuple-element.61), channel_id=1, source_target_pairs={{0,6},{1,7},{2,4},{3,5},{4,2},{5,3},{6,0},{7,1},{8,14},{9,15},{10,... | collective-permute-start | bytes 393224 | tf_op jit(solution)/shard_map/ppermute | solution.py:323
  78.7 7.7 %collective-permute-start.25 = (bf16[128,512]{1,0:T(8,128)(2,1)S(1)}, bf16[128,512]{1,0:T(8,128)(2,1)S(1)}, u32[]{:S(2)}, u32[]{:S(2)}) collective-permute-start(bf16[128,512]{1,0:T(8,128)(2,1)S(1)} %get-tuple-element.62), channel_id=1, source_target_pairs={{0,2},{1,3},{2,0},{3,1},{4,6},{5,7},{6,4},{7,5},{8,10},{9,11},{10,... | collective-permute-start | bytes 393224 | tf_op jit(solution)/shard_map/ppermute | solution.py:323
  80.1 16.4 %collective-permute-start.26 = (bf16[128,512]{1,0:T(8,128)(2,1)S(1)}, bf16[128,512]{1,0:T(8,128)(2,1)S(1)}, u32[]{:S(2)}, u32[]{:S(2)}) collective-permute-start(bf16[128,512]{1,0:T(8,128)(2,1)S(1)} %get-tuple-element.63), channel_id=1, source_target_pairs={{0,4},{1,5},{2,6},{3,7},{4,0},{5,1},{6,2},{7,3},{8,12},{9,13},{10,... | collective-permute-start | bytes 393224 | tf_op jit(solution)/shard_map/ppermute | solution.py:323
  96.5 6.7 %collective-permute-start.27 = (bf16[128,512]{1,0:T(8,128)(2,1)S(1)}, bf16[128,512]{1,0:T(8,128)(2,1)S(1)}, u32[]{:S(2)}, u32[]{:S(2)}) collective-permute-start(bf16[128,512]{1,0:T(8,128)(2,1)S(1)} %add_convert_fusion.1), channel_id=1, source_target_pairs={{0,8},{1,9},{2,10},{3,11},{4,12},{5,13},{6,14},{7,15},{8,0},{9,1},... | collective-permute-start | bytes 393224 | tf_op jit(solution)/shard_map/ppermute | solution.py:323
  100.0 14.8 %collective-permute-start.33 = (bf16[2048,128]{1,0:T(8,128)(2,1)S(1)}, bf16[2048,128]{1,0:T(8,128)(2,1)S(1)}, u32[]{:S(2)}, u32[]{:S(2)}) collective-permute-start(bf16[2048,128]{1,0:T(8,128)(2,1)S(1)} %get-tuple-element.64.e0), channel_id=1, source_target_pairs={{0,2},{1,3},{2,0},{3,1},{4,6},{5,7},{6,4},{7,5},{8,10},{9,11},{10,... | collective-permute-start | bytes 1572872 | tf_op jit(solution)/shard_map/ppermute | solution.py:323
  100.8 25.2 %collective-permute-start.35 = (bf16[2048,128]{1,0:T(8,128)(2,1)S(1)}, bf16[2048,128]{1,0:T(8,128)(2,1)S(1)}, u32[]{:S(2)}, u32[]{:S(2)}) collective-permute-start(bf16[2048,128]{1,0:T(8,128)(2,1)S(1)} %collective-permute-done.34.e2), channel_id=1, source_target_pairs={{0,2},{1,3},{2,0},{3,1},{4,6},{5,7},{6,4},{7,5},{8,10},{9,11},{10,... | collective-permute-start | bytes 1572872 | tf_op jit(solution)/shard_map/ppermute | solution.py:323
  103.3 6.1 %collective-permute-start.28 = (bf16[128,512]{1,0:T(8,128)(2,1)S(1)}, bf16[128,512]{1,0:T(8,128)(2,1)S(1)}, u32[]{:S(2)}, u32[]{:S(2)}) collective-permute-start(bf16[128,512]{1,0:T(8,128)(2,1)S(1)} %add_convert_fusion), channel_id=1, source_target_pairs={{0,16},{1,17},{2,18},{3,19},{4,20},{5,21},{6,22},{7,23},{8,24},{9,... | collective-permute-start | bytes 393224 | tf_op jit(solution)/shard_map/ppermute | solution.py:323
  104.9 5.5 %collective-permute-start.32 = (bf16[64,2688]{1,0:T(8,128)(2,1)S(1)}, bf16[64,2688]{1,0:T(8,128)(2,1)S(1)}, u32[]{:S(2)}, u32[]{:S(2)}) collective-permute-start(bf16[64,2688]{1,0:T(8,128)(2,1)S(1)} %pad_maximum_fusion.w0.own_ref), channel_id=1, source_target_pairs={{0,1},{1,0},{2,3},{3,2},{4,5},{5,4},{6,7},{7,6},{8,9},{9,8},{10,11... | collective-permute-start | bytes 1032200 | tf_op jit(solution)/shard_map/ppermute | solution.py:323
  109.5 19.1 %collective-permute-start.29 = (bf16[128,512]{1,0:T(8,128)(2,1)S(1)}, bf16[128,512]{1,0:T(8,128)(2,1)S(1)}, u32[]{:S(2)}, u32[]{:S(2)}) collective-permute-start(bf16[128,512]{1,0:T(8,128)(2,1)S(1)} %multiply_convert_fusion.p0), channel_id=1, source_target_pairs={{0,2},{1,3},{2,0},{3,1},{4,6},{5,7},{6,4},{7,5},{8,10},{9,11},{10,... | collective-permute-start | bytes 393224 | tf_op jit(solution)/shard_map/ppermute | solution.py:323
  110.4 18.2 %collective-permute-start.30 = (bf16[128,512]{1,0:T(8,128)(2,1)S(1)}, bf16[128,512]{1,0:T(8,128)(2,1)S(1)}, u32[]{:S(2)}, u32[]{:S(2)}) collective-permute-start(bf16[128,512]{1,0:T(8,128)(2,1)S(1)} %multiply_convert_fusion.p0), channel_id=1, source_target_pairs={{0,4},{1,5},{2,6},{3,7},{4,0},{5,1},{6,2},{7,3},{8,12},{9,13},{10,... | collective-permute-start | bytes 393224 | tf_op jit(solution)/shard_map/ppermute | solution.py:323
  114.8 15.5 %collective-permute-start.31 = (bf16[128,512]{1,0:T(8,128)(2,1)S(1)}, bf16[128,512]{1,0:T(8,128)(2,1)S(1)}, u32[]{:S(2)}, u32[]{:S(2)}) collective-permute-start(bf16[128,512]{1,0:T(8,128)(2,1)S(1)} %multiply_convert_fusion.p0), channel_id=1, source_target_pairs={{0,6},{1,7},{2,4},{3,5},{4,2},{5,3},{6,0},{7,1},{8,14},{9,15},{10,... | collective-permute-start | bytes 393224 | tf_op jit(solution)/shard_map/ppermute | solution.py:323
  131.4 26.0 %collective-permute-start.36 = (bf16[80,2560]{1,0:T(8,128)(2,1)S(1)}, bf16[80,2560]{1,0:T(8,128)(2,1)S(1)}, u32[]{:S(2)}, u32[]{:S(2)}) collective-permute-start(bf16[80,2560]{1,0:T(8,128)(2,1)S(1)} %get-tuple-element.72), channel_id=1, source_target_pairs={{0,1},{1,0},{2,3},{3,2},{4,5},{5,4},{6,7},{7,6},{8,9},{9,8},{10,11... | collective-permute-start | bytes 1228808 | tf_op jit(solution)/shard_map/ppermute | solution.py:323
  131.5 26.9 %collective-permute-start.38 = (bf16[100,2048]{1,0:T(8,128)(2,1)S(1)}, bf16[100,2048]{1,0:T(8,128)(2,1)S(1)}, u32[]{:S(2)}, u32[]{:S(2)}) collective-permute-start(bf16[100,2048]{1,0:T(8,128)(2,1)S(1)} %get-tuple-element.79), channel_id=1, source_target_pairs={{0,1},{1,0},{2,3},{3,2},{4,5},{5,4},{6,7},{7,6},{8,9},{9,8},{10,11... | collective-permute-start | bytes 1228808 | tf_op jit(solution)/shard_map/ppermute | solution.py:323
  135.9 4.8 %collective-permute-start.20 = (bf16[128,100]{1,0:T(8,128)(2,1)S(1)}, bf16[128,100]{1,0:T(8,128)(2,1)S(1)}, u32[]{:S(2)}, u32[]{:S(2)}) collective-permute-start(bf16[128,100]{1,0:T(8,128)(2,1)S(1)} %get-tuple-element.55), channel_id=1, source_target_pairs={{0,6},{1,7},{2,4},{3,5},{4,2},{5,3},{6,0},{7,1},{8,14},{9,15},{10,... | collective-permute-start | bytes 76808 | tf_op jit(solution)/shard_map/ppermute | solution.py:323
  149.1 7.7 %collective-permute-start.23 = (bf16[32,100]{1,0:T(8,128)(2,1)S(1)}, bf16[32,100]{1,0:T(8,128)(2,1)S(1)}, u32[]{:S(2)}, u32[]{:S(2)}) collective-permute-start(bf16[32,100]{1,0:T(8,128)(2,1)S(1)} %add_convert_fusion.4), channel_id=1, source_target_pairs={{0,0},{1,16},{2,4},{3,20},{4,8},{5,24},{6,12},{7,28},{8,1},{9,17},... | collective-permute-start | bytes 19208 | tf_op jit(solution)/shard_map/ppermute | solution.py:323
  (11 other events, 137.0 us)
